TPU v7x, 32 devices: a whole 2x2x4 slice. The times are simulated.
32 devices in a mesh: dp: 8 (over z, x), tok: 4 (over y, core).
Axes of the slice: x: 2, y: 2, z: 4, core: 2. Of those that a mesh axis runs over, the one named last changes fastest.
Arguments:
- inputs: bfloat16 [128, 200, 384], P(('dp', 'tok')), may hold values from -6 to 6
- cotangent: bfloat16 [128, 200, 384], P(('dp', 'tok')), may hold values from -6 to 6
- lengths: int32 [128], P('dp'), may hold values from 1 to 198, 12672 in all
- w_qkv: float32 [2, 384, 1152], P(None, None, 'dp'), may hold values from -0.3125 to 0.3125
- w_proj: float32 [2, 384, 384], P(None, None, 'dp'), may hold values from -0.875 to 0.875
- w_fc1: float32 [2, 384, 1536], P(None, None, 'dp'), may hold values from -0.3125 to 0.3125
- w_fc2: float32 [2, 1536, 384], P(None, 'dp'), may hold values from -0.15625 to 0.15625
- norm_gains: float32 [2, 2, 384], P(None, None, 'dp'), may hold values from 0.5 to 1.5
- biases: float32 [2, 3840], P(None, 'dp'), may hold values from -1.75 to 1.75
- mom_qkv: float32 [2, 2, 384, 1152], P(None, None, None, 'dp'), as said below
- mom_proj: float32 [2, 2, 384, 384], P(None, None, None, 'dp'), as said below
- mom_fc1: float32 [2, 2, 384, 1536], P(None, None, None, 'dp'), as said below
- mom_fc2: float32 [2, 2, 1536, 384], P(None, None, 'dp'), as said below
- mom_gains: float32 [2, 2, 2, 384], P(None, None, None, 'dp'), as said below
- mom_biases: float32 [2, 2, 3840], P(None, None, 'dp'), as said below
Outputs:
- layer_out: bfloat16 [128, 200, 384], P(('dp', 'tok'))
- input_grad: float32 [128, 200, 384], P(('dp', 'tok'))
- grad_norm: float32 [], replicated
- state_qkv: float32 [2, 2, 384, 1152], P(None, None, None, 'dp')
- state_proj: float32 [2, 2, 384, 384], P(None, None, None, 'dp')
- state_fc1: float32 [2, 2, 384, 1536], P(None, None, None, 'dp')
- state_fc2: float32 [2, 2, 1536, 384], P(None, None, 'dp')
- state_gains: float32 [2, 2, 2, 384], P(None, None, None, 'dp')
- state_biases: float32 [2, 2, 3840], P(None, None, 'dp')
- second_moments: float32 [3548160], P('dp')
Inputs may be any that keep to these rules, and one draw needn't show every extreme that they name: Sequence i keeps its first lengths[i] slots; some sequence keeps all 198. `mom_qkv`: index 0 holds the first moment, index 1 the second moment, which is positive. `mom_proj`: index 0 holds the first moment, index 1 the second moment, which is positive. `mom_fc1`: index 0 holds the first moment, index 1 the second moment, which is positive. `mom_fc2`: index 0 holds the first moment, index 1 the second moment, which is positive. `mom_gains`: index 0 holds the first moment, index 1 the second moment, which is positive. `mom_biases`: index 0 holds the first moment, index 1 the second moment, which is positive.
All inputs are finite; a program needn't handle non-finite values. No bound on the sum of `lengths` on one device may be relied on, other than what follows from the above.
Results may differ from a plain program's by a relative error of at most 0.018.
The roundings to bfloat16 on the way count: a program that leaves them out, or rounds other values in their place, can miss the bound.
Values may be sent and summed in bfloat16 or wider, within the bound.
No kernel may reach another device: no remote copies, remote signals or barrier semaphores. Data moves between devices by JAX's collectives and lax.ppermute only.
A program may use at most 128 MiB of HBM per device.

v0:
```python
import math

import jax
import jax.numpy as jnp
from jax import lax
from jax.sharding import PartitionSpec as P

D = 384
HEADS = 6
HD = 64
FF = 1536
LAYERS = 2
STEP = 10


HALF_ROOT = 0.7071067811865476
INV_ROOT_TAU = 0.3989422804014327


def normalize(hidden):
    row_mean = jnp.mean(hidden, -1, keepdims=True)
    centered = hidden - row_mean
    variance = jnp.mean(centered * centered, -1, keepdims=True)
    inverse = lax.rsqrt(variance + 1e-06)
    return (centered * inverse, inverse)


def norm_back(grad_n, normed, inverse):
    first_mean = jnp.mean(grad_n, -1, keepdims=True)
    second_mean = jnp.mean(grad_n * normed, -1, keepdims=True)
    return inverse * (grad_n - first_mean - normed * second_mean)


def gelu_slope(pre_act):
    return (
        0.5 * (1.0 + lax.erf(pre_act * HALF_ROOT))
        + pre_act * jnp.exp(-0.5 * pre_act * pre_act) * INV_ROOT_TAU
    )


def spread_heads(tensor, axis):
    first = lax.slice_in_dim(tensor, 0, 5, axis=axis)
    last = lax.slice_in_dim(tensor, 5, 6, axis=axis)
    empty = jnp.zeros_like(last)
    return jnp.concatenate([first, empty, last, empty], axis)


def pick_heads(tensor, axis):
    first = lax.slice_in_dim(tensor, 0, 5, axis=axis)
    last = lax.slice_in_dim(tensor, 6, 7, axis=axis)
    return jnp.concatenate([first, last], axis)


def qkv_to_heads(packed):
    seq_count, slot_total = (packed.shape[0], packed.shape[1])
    sending = spread_heads(packed, 3).reshape(seq_count, slot_total, 3, 4, 2 * HD)
    arrived = lax.all_to_all(sending, "tok", split_axis=3, concat_axis=0, tiled=True)
    return arrived.reshape(4 * seq_count, slot_total, 3, 2, HD)


def out_to_rows(attended):
    batch_size, slot_total = (attended.shape[0], attended.shape[1])
    sending = attended.reshape(batch_size, slot_total, 1, 2 * HD)
    arrived = lax.all_to_all(sending, "tok", split_axis=0, concat_axis=2, tiled=True)
    return pick_heads(arrived.reshape(batch_size // 4, slot_total, 8, HD), 2)


def dout_to_heads(grad_rows):
    seq_count, slot_total = (grad_rows.shape[0], grad_rows.shape[1])
    sending = spread_heads(grad_rows, 2).reshape(seq_count, slot_total, 4, 2 * HD)
    arrived = lax.all_to_all(sending, "tok", split_axis=2, concat_axis=0, tiled=True)
    return arrived.reshape(4 * seq_count, slot_total, 2, HD)


def grads_to_rows(stacked):
    batch_size, slot_total = (stacked.shape[0], stacked.shape[1])
    sending = stacked.reshape(batch_size, slot_total, 3, 1, 2 * HD)
    arrived = lax.all_to_all(sending, "tok", split_axis=0, concat_axis=3, tiled=True)
    return pick_heads(arrived.reshape(batch_size // 4, slot_total, 3, 8, HD), 3)


def score_block(query_b, key_b, lens_block):
    scores = (
        jnp.einsum("bqhd,bkhd->bhqk", query_b, key_b, preferred_element_type=jnp.float32) * 0.125
    )
    key_mask = jnp.arange(key_b.shape[1])[None, :] < lens_block[:, None]
    return jnp.where(key_mask[:, None, None, :], scores, -1e30)


def forward_block(packed):
    stacked, lens_block = packed
    query_b = stacked[:, :, 0]
    key_b = stacked[:, :, 1]
    value_b = stacked[:, :, 2]
    scores = score_block(query_b, key_b, lens_block)
    row_max = jnp.max(scores, -1, keepdims=True)
    exp_part = jnp.exp(scores - row_max)
    summed = jnp.sum(exp_part, -1, keepdims=True)
    prob_low = (exp_part / summed).astype(jnp.bfloat16)
    result = jnp.einsum("bhqk,bkhd->bqhd", prob_low, value_b, preferred_element_type=jnp.float32)
    return (result.astype(jnp.bfloat16), (row_max + jnp.log(summed))[..., 0])


def backward_block(packed):
    stacked, lse_block, dout_block, lens_block = packed
    query_b = stacked[:, :, 0]
    key_b = stacked[:, :, 1]
    value_b = stacked[:, :, 2]
    scores = score_block(query_b, key_b, lens_block)
    prob_full = jnp.exp(scores - lse_block[..., None])
    grad_v = jnp.einsum(
        "bhqk,bqhd->bkhd",
        prob_full.astype(jnp.bfloat16),
        dout_block,
        preferred_element_type=jnp.float32,
    )
    grad_p = jnp.einsum("bqhd,bkhd->bhqk", dout_block, value_b, preferred_element_type=jnp.float32)
    inner_sum = jnp.sum(prob_full * grad_p, -1, keepdims=True)
    grad_s = (prob_full * (grad_p - inner_sum)).astype(jnp.bfloat16)
    grad_q = (
        jnp.einsum("bhqk,bkhd->bqhd", grad_s, key_b, preferred_element_type=jnp.float32) * 0.125
    )
    grad_k = (
        jnp.einsum("bhqk,bqhd->bkhd", grad_s, query_b, preferred_element_type=jnp.float32) * 0.125
    )
    return jnp.stack([grad_q, grad_k, grad_v], 2).astype(jnp.bfloat16)


def run_blocks(block_fn, arrays):
    batch_size = arrays[0].shape[0]
    folded = tuple((entry.reshape((batch_size // 4, 4) + entry.shape[1:]) for entry in arrays))
    result = lax.map(block_fn, folded)

    def unfold(folded_part):
        return folded_part.reshape((batch_size,) + folded_part.shape[2:])

    return jax.tree.map(unfold, result)


def sum_squares(tensors):
    return sum((jnp.sum(entry * entry) for entry in tensors))


def adamw(weight, moments, clipped, rate, decay):
    first_mom = 0.9 * moments[0] + 0.1 * clipped
    second_mom = 0.999 * moments[1] + 0.001 * clipped * clipped
    fixed_first = first_mom / (1.0 - 0.9**STEP)
    fixed_second = second_mom / (1.0 - 0.999**STEP)
    new_weight = weight - rate * (fixed_first / (jnp.sqrt(fixed_second) + 1e-08) + decay * weight)
    return (jnp.stack([new_weight, first_mom]), second_mom)


def on_device(
    inputs,
    cotangent,
    lengths,
    w_qkv,
    w_proj,
    w_fc1,
    w_fc2,
    norm_gains,
    biases,
    mom_qkv,
    mom_proj,
    mom_fc1,
    mom_fc2,
    mom_gains,
    mom_biases,
):
    full_qkv, full_proj, full_fc1, full_fc2, full_gains, full_biases = (
        lax.all_gather(w_qkv.astype(jnp.bfloat16), "dp", axis=2, tiled=True),
        lax.all_gather(w_proj.astype(jnp.bfloat16), "dp", axis=2, tiled=True),
        lax.all_gather(w_fc1.astype(jnp.bfloat16), "dp", axis=2, tiled=True),
        lax.all_gather(w_fc2.astype(jnp.bfloat16), "dp", axis=1, tiled=True),
        lax.all_gather(norm_gains.astype(jnp.bfloat16), "dp", axis=2, tiled=True),
        lax.all_gather(biases.astype(jnp.bfloat16), "dp", axis=1, tiled=True),
    )
    seq_count = inputs.shape[0]
    slot_total = inputs.shape[1]
    row_count = seq_count * slot_total
    tok_index = lax.axis_index("tok")
    own_lengths = lax.dynamic_slice_in_dim(lengths, tok_index * seq_count, seq_count, 0)
    positions = jnp.arange(slot_total)
    valid = (positions[None, :] < own_lengths[:, None]).reshape(row_count, 1)
    hidden = inputs.astype(jnp.float32).reshape(row_count, D)
    saved = []
    for layer_id in range(LAYERS):
        q_weight = full_qkv[layer_id]
        o_weight = full_proj[layer_id]
        up_weight = full_fc1[layer_id]
        down_weight = full_fc2[layer_id]
        gain_rows = full_gains[layer_id].astype(jnp.float32)
        bias_row = full_biases[layer_id].astype(jnp.float32)
        norm_first, inv_first = normalize(hidden)
        a_first = (norm_first * gain_rows[0] + bias_row[0:D]).astype(jnp.bfloat16)
        qkv_bias = jnp.concatenate(
            [bias_row[D : 2 * D], jnp.zeros((D,), jnp.float32), bias_row[2 * D : 3 * D]]
        )
        qkv = jnp.dot(a_first, q_weight, preferred_element_type=jnp.float32) + qkv_bias
        qkv = qkv.astype(jnp.bfloat16).reshape(seq_count, slot_total, 3, HEADS, HD)
        head_qkv = qkv_to_heads(qkv)
        attended, lse_all = run_blocks(forward_block, (head_qkv, lengths))
        att_rows = out_to_rows(attended).reshape(row_count, D)
        mid_hidden = (
            hidden
            + jnp.dot(att_rows, o_weight, preferred_element_type=jnp.float32)
            + bias_row[3 * D : 4 * D]
        )
        norm_second, inv_second = normalize(mid_hidden)
        a_second = (norm_second * gain_rows[1] + bias_row[4 * D : 5 * D]).astype(jnp.bfloat16)
        pre_act = (
            jnp.dot(a_second, up_weight, preferred_element_type=jnp.float32) + bias_row[6 * D :]
        )
        activated = jax.nn.gelu(pre_act, approximate=False).astype(jnp.bfloat16)
        hidden = (
            mid_hidden
            + jnp.dot(activated, down_weight, preferred_element_type=jnp.float32)
            + bias_row[5 * D : 6 * D]
        )
        saved.append(
            (
                norm_first,
                inv_first,
                a_first,
                head_qkv,
                lse_all,
                att_rows,
                norm_second,
                inv_second,
                a_second,
                pre_act,
                activated,
            )
        )
    layer_out = jnp.where(valid, hidden, 0.0).astype(jnp.bfloat16).reshape(inputs.shape)
    grad_h = cotangent.astype(jnp.float32).reshape(row_count, D) * valid.astype(jnp.float32)
    list_qkv = [None] * LAYERS
    list_proj = [None] * LAYERS
    list_fc1 = [None] * LAYERS
    list_fc2 = [None] * LAYERS
    list_gains = [None] * LAYERS
    list_biases = [None] * LAYERS
    for layer_id in range(LAYERS - 1, -1, -1):
        (
            norm_first,
            inv_first,
            a_first,
            head_qkv,
            lse_all,
            att_rows,
            norm_second,
            inv_second,
            a_second,
            pre_act,
            activated,
        ) = saved[layer_id]
        q_weight = full_qkv[layer_id]
        o_weight = full_proj[layer_id]
        up_weight = full_fc1[layer_id]
        down_weight = full_fc2[layer_id]
        gain_rows = full_gains[layer_id].astype(jnp.float32)
        grad_m = grad_h.astype(jnp.bfloat16)
        list_fc2[layer_id] = jnp.einsum(
            "rf,rd->fd", activated, grad_m, preferred_element_type=jnp.float32
        )
        bias_fc2 = jnp.sum(grad_m, 0, dtype=jnp.float32)
        grad_act = jnp.einsum("rd,fd->rf", grad_m, down_weight, preferred_element_type=jnp.float32)
        grad_up = (grad_act * gelu_slope(pre_act)).astype(jnp.bfloat16)
        list_fc1[layer_id] = jnp.einsum(
            "rd,rf->df", a_second, grad_up, preferred_element_type=jnp.float32
        )
        bias_fc1 = jnp.sum(grad_up, 0, dtype=jnp.float32)
        grad_a2 = jnp.einsum("rf,df->rd", grad_up, up_weight, preferred_element_type=jnp.float32)
        gain_second = jnp.sum(grad_a2 * norm_second, 0)
        bias_ln2 = jnp.sum(grad_a2, 0)
        grad_mid = grad_h + norm_back(grad_a2 * gain_rows[1], norm_second, inv_second)
        grad_p = grad_mid.astype(jnp.bfloat16)
        list_proj[layer_id] = jnp.einsum(
            "rd,re->de", att_rows, grad_p, preferred_element_type=jnp.float32
        )
        bias_proj = jnp.sum(grad_p, 0, dtype=jnp.float32)
        grad_att = jnp.einsum("re,de->rd", grad_p, o_weight, preferred_element_type=jnp.float32)
        grad_att = grad_att.astype(jnp.bfloat16).reshape(seq_count, slot_total, HEADS, HD)
        head_dout = dout_to_heads(grad_att)
        head_grads = run_blocks(backward_block, (head_qkv, lse_all, head_dout, lengths))
        grad_qkv = grads_to_rows(head_grads).reshape(row_count, 3 * D)
        list_qkv[layer_id] = jnp.einsum(
            "rd,rc->dc", a_first, grad_qkv, preferred_element_type=jnp.float32
        )
        bias_q = jnp.sum(grad_qkv[:, 0:D], 0, dtype=jnp.float32)
        bias_v = jnp.sum(grad_qkv[:, 2 * D : 3 * D], 0, dtype=jnp.float32)
        grad_a1 = jnp.einsum("rc,dc->rd", grad_qkv, q_weight, preferred_element_type=jnp.float32)
        gain_first = jnp.sum(grad_a1 * norm_first, 0)
        bias_ln1 = jnp.sum(grad_a1, 0)
        grad_h = grad_mid + norm_back(grad_a1 * gain_rows[0], norm_first, inv_first)
        list_gains[layer_id] = jnp.stack([gain_first, gain_second])
        list_biases[layer_id] = jnp.concatenate(
            [bias_ln1, bias_q, bias_v, bias_proj, bias_ln2, bias_fc2, bias_fc1]
        )
    input_grad = grad_h.reshape(inputs.shape)
    grad_qkv_all = jnp.stack(list_qkv)
    grad_proj_all = jnp.stack(list_proj)
    grad_fc1_all = jnp.stack(list_fc1)
    grad_fc2_all = jnp.stack(list_fc2)
    grad_gain_all = jnp.stack(list_gains)
    grad_bias_all = jnp.stack(list_biases)
    masters = (w_qkv, w_proj, w_fc1, w_fc2, norm_gains, biases)
    shard_dims = (2, 2, 2, 1, 2, 1)
    dp_index = lax.axis_index("dp")
    summed = lax.psum(
        (grad_qkv_all, grad_proj_all, grad_fc1_all, grad_fc2_all, grad_gain_all, grad_bias_all),
        ("dp", "tok"),
    )
    squares = sum_squares(summed)
    shares = tuple(
        (
            lax.dynamic_slice_in_dim(
                summed_part, dp_index * owner.shape[shard_dim], owner.shape[shard_dim], shard_dim
            )
            for summed_part, owner, shard_dim in zip(summed, masters, shard_dims)
        )
    )
    grad_norm = jnp.sqrt(squares)
    limit = 0.25 * math.sqrt(LAYERS * (4 * D * D + 2 * D * FF + 8 * D + FF))
    factor = jnp.minimum(1.0, limit / (grad_norm + 1e-06))
    state_qkv, second_qkv = adamw(w_qkv, mom_qkv, shares[0] * factor, 0.08, 0.05)
    state_proj, second_proj = adamw(w_proj, mom_proj, shares[1] * factor, 0.08, 0.05)
    state_fc1, second_fc1 = adamw(w_fc1, mom_fc1, shares[2] * factor, 0.08, 0.05)
    state_fc2, second_fc2 = adamw(w_fc2, mom_fc2, shares[3] * factor, 0.08, 0.05)
    state_gains, second_gains = adamw(norm_gains, mom_gains, shares[4] * factor, 0.4, 0.0)
    state_biases, second_biases = adamw(biases, mom_biases, shares[5] * factor, 0.4, 0.0)
    second_moments = jnp.concatenate(
        [
            second_qkv.reshape(-1),
            second_proj.reshape(-1),
            second_fc1.reshape(-1),
            second_fc2.reshape(-1),
            second_gains.reshape(-1),
            second_biases.reshape(-1),
        ]
    )
    return (
        layer_out,
        input_grad,
        grad_norm,
        state_qkv,
        state_proj,
        state_fc1,
        state_fc2,
        state_gains,
        state_biases,
        second_moments,
    )


def solution(mesh):
    placed = (
        P(("dp", "tok"), None, None),
        P(("dp", "tok"), None, None),
        P("dp"),
        P(None, None, "dp"),
        P(None, None, "dp"),
        P(None, None, "dp"),
        P(None, "dp", None),
        P(None, None, "dp"),
        P(None, "dp"),
        P(None, None, None, "dp"),
        P(None, None, None, "dp"),
        P(None, None, None, "dp"),
        P(None, None, "dp", None),
        P(None, None, None, "dp"),
        P(None, None, "dp"),
    )
    return jax.shard_map(
        on_device,
        mesh=mesh,
        in_specs=placed,
        out_specs=(
            P(("dp", "tok"), None, None),
            P(("dp", "tok"), None, None),
            P(),
            P(None, None, None, "dp"),
            P(None, None, None, "dp"),
            P(None, None, None, "dp"),
            P(None, None, "dp", None),
            P(None, None, None, "dp"),
            P(None, None, "dp"),
            P("dp"),
        ),
        check_vma=False,
    )
```

profile of v0, /device:TPU:0, one launch (start us, length us, event | category | flops | bytes accessed | tf_op | source)
XLA Modules:
  0.0 898.1 jit_solution(4694405918327446632)
XLA Ops:
  9.7 27.9 %all-gather = bf16[8,480,2]{1,2,0:T(2,128)(2,1)S(1)} all-gather(bf16[1,480,2]{1,2,0:T(2,128)(2,1)S(1)} %convert_bitcast_fusion), channel_id=1, replica_groups=mesh['dp'=8,'tok'=4] {'dp'}, dimensions={0}, use_global_device_ids=true | all-gather | bytes 17280 | tf_op jit(solution)/shard_map/all_gather | solution.py:176
  38.5 31.1 %all_gather.18 = bf16[2,2,384]{1,0,2:T(2,128)(2,1)S(1)} all-gather(bf16[2,2,48]{1,0,2:T(2,128)(2,1)S(1)} %copy.330), channel_id=1, replica_groups=mesh['dp'=8,'tok'=4] {'dp'}, dimensions={2}, use_global_device_ids=true | all-gather | bytes 3456 | tf_op jit(solution)/shard_map/all_gather | solution.py:175
  73.5 4.9 slice_reduce_fusion
  83.9 5.7 reshape.586
  90.7 2.9 pad_maximum_fusion.5
  93.6 3.6 copy.334
  97.2 4.6 all-to-all-start
  103.4 28.1 %all-to-all-done = bf16[4,200,3,4,128]{4,1,2,0,3:T(8,128)(2,1)} async-done(((bf16[4,200,3,4,128]{4,1,2,0,3:T(8,128)(2,1)}), bf16[4,200,3,4,128]{4,1,2,0,3:T(8,128)(2,1)}, u32[]{:S(2)}, u32[]{:S(2)}) %all-to-all-start) | async-done | bytes 2457632 | tf_op jit(solution)/shard_map/all_to_all | solution.py:57
  131.5 3.0 copy.392
  136.3 13.3 %while.44 = (s32[]{:T(128)}, bf16[4,4,200,2,64]{2,4,3,1,0:T(8,128)(2,1)}, f32[4,4,2,200]{3,2,1,0:T(2,128)}, bf16[4,4,200,3,2,64]{2,5,4,1,3,0:T(8,128)(2,1)S(1)}, s32[4,4]{1,0:T(4,128)}, /*index=5*/s32[]{:T(128)}) while((s32[]{:T(128)}, bf16[4,4,200,2,64]{2,4,3,1,0:T(8,128)(2,1)}, f32[4,4,2,200]{3,2,1,0:T(2,128)}, ...), condition=%wide.region_5.6_spmd, body=%wide.region_2.5_spmd.sunk | while | flops 84581600 | bytes 6535325 | solution.py:132
  149.6 2.9 copy.337
  152.5 4.2 all-to-all-start.1
  160.9 33.1 %all_gather.21 = bf16[2,384,384]{1,2,0:T(8,128)(2,1)S(1)} all-gather(bf16[2,384,48]{1,2,0:T(8,128)(2,1)S(1)} %convert_element_type.200), channel_id=1, replica_groups=mesh['dp'=8,'tok'=4] {'dp'}, dimensions={2}, use_global_device_ids=true | all-gather | bytes 663552 | tf_op jit(solution)/shard_map/all_gather | solution.py:172
  198.3 14.6 %fusion.38 = (bf16[800,1536]{1,0:T(8,128)(2,1)}, f32[800,1536]{1,0:T(8,128)}) fusion(f32[1536]{0:T(1024)S(1)} %get-tuple-element.494, bf16[2,384,1536]{1,2,0:T(8,128)(2,1)} %all-gather.7.cloned.1.call-done, f32[800,384]{1,0:T(8,128)S(1)} %get-tuple-element.476, f32[384]{0:T(512)S(1)} %copy-done.70, f32[384]{0:T(512)S(1)} %copy-done.66, ...), kind=kOutput, calls=%fused_computation.94 | convolution fusion | flops 1026355200 | bytes 9796864 | tf_op jit(solution)/shard_map/dot_general | solution.py:212
  214.7 3.7 fusion.121
  223.2 5.7 reshape.591
  229.9 2.9 pad_maximum_fusion.4
  232.8 13.8 %copy.342 = bf16[4,200,3,4,128]{4,1,2,0,3:T(8,128)(2,1)} copy(bf16[4,200,3,4,128]{1,0,4,3,2:T(4,128)(2,1)S(1)} %bitcast.482) | data formatting | bytes 4915200 | tf_op jit(solution)/shard_map/reshape | solution.py:56
  246.6 4.6 all-to-all-start.2
  251.2 29.6 %all-to-all-done.2 = bf16[4,200,3,4,128]{4,1,2,0,3:T(8,128)(2,1)} async-done(((bf16[4,200,3,4,128]{4,1,2,0,3:T(8,128)(2,1)}), bf16[4,200,3,4,128]{4,1,2,0,3:T(8,128)(2,1)}, u32[]{:S(2)}, u32[]{:S(2)}) %all-to-all-start.2) | async-done | bytes 2457632 | tf_op jit(solution)/shard_map/all_to_all | solution.py:57
  280.8 3.0 copy.395
  285.0 8.3 while.45
  295.5 4.2 all-to-all-start.3
  300.0 2.7 convert_reduce_fusion.6
  302.7 9.1 %all-to-all-done.3 = bf16[16,200,1,128]{3,1,2,0:T(8,128)(2,1)} async-done(((bf16[16,200,1,128]{3,1,2,0:T(8,128)(2,1)}), bf16[16,200,1,128]{3,1,2,0:T(8,128)(2,1)}, u32[]{:S(2)}, u32[]{:S(2)}) %all-to-all-start.3) | async-done | bytes 819232 | tf_op jit(solution)/shard_map/all_to_all | solution.py:64
  317.8 2.7 reshape.594
  323.4 12.8 %fusion.41 = (bf16[800,1536]{1,0:T(8,128)(2,1)}, f32[800,1536]{1,0:T(8,128)S(1)}) fusion(f32[1536]{0:T(1024)S(1)} %copy-done.85, bf16[2,384,1536]{1,2,0:T(8,128)(2,1)S(1)} %copy-done.111, f32[800,384]{1,0:T(8,128)S(1)} %get-tuple-element.482, f32[384]{0:T(512)S(1)} %copy-done.72, f32[384]{0:T(512)S(1)} %copy-done.65, f32[800]{0:T(1024)S(1)} %add_rsqrt_fusion, ...), kind=kOutput, calls=%fused_computation.97 | convolution fusion | flops 1026355200 | bytes 9801728 | tf_op jit(solution)/shard_map/dot_general | solution.py:212
  336.1 4.3 convert_reduce_fusion
  349.8 3.3 reshape.597
  358.5 4.2 all-to-all-start.4
  362.7 12.1 %all-to-all-done.4 = bf16[4,200,4,128]{3,1,0,2:T(8,128)(2,1)} async-done(((bf16[4,200,4,128]{3,1,0,2:T(8,128)(2,1)}), bf16[4,200,4,128]{3,1,0,2:T(8,128)(2,1)}, u32[]{:S(2)}, u32[]{:S(2)}) %all-to-all-start.4) | async-done | bytes 819232 | tf_op jit(solution)/shard_map/all_to_all | solution.py:71
  379.1 23.6 %while.46 = (s32[]{:T(128)}, bf16[4,4,200,3,2,64]{2,5,4,3,1,0:T(8,128)(2,1)}, bf16[4,4,200,3,2,64]{2,5,4,1,3,0:T(8,128)(2,1)S(1)}, s32[4,4]{1,0:T(4,128)S(1)}, f...) while((s32[]{:T(128)}, bf16[4,4,200,3,2,64]{2,5,4,3,1,0:T(8,128)(2,1)}, ...), condition=%wide.region_20.21_spmd, body=%wide.region_18.20_spmd.sunk | while | flops 208805600 | bytes 15433129 | solution.py:132
  402.7 4.6 copy.354
  407.2 4.7 all-to-all-start.5
  411.9 4.7 convolution_bitcast_fusion.2
  416.6 24.9 %all-to-all-done.5 = bf16[16,200,3,1,128]{4,1,3,2,0:T(8,128)(2,1)} async-done(((bf16[16,200,3,1,128]{4,1,3,2,0:T(8,128)(2,1)}), bf16[16,200,3,1,128]{4,1,3,2,0:T(8,128)(2,1)}, u32[]{:S(2)}, u32[]{:S(2)}) %all-to-all-start.5) | async-done | bytes 2457632 | tf_op jit(solution)/shard_map/all_to_all | solution.py:78
  441.6 4.6 copy.355
  449.3 3.5 copy.356
  452.7 5.5 reshape.600
  458.2 4.1 multiply_reduce_fusion.6
  464.0 5.9 convert_reduce_fusion.1
  476.0 2.8 reshape.601
  482.5 4.2 all-to-all-start.6
  486.7 5.1 convolution_bitcast_fusion
  494.9 3.9 all-to-all-done.6
  502.2 23.0 %while.47 = (s32[]{:T(128)}, bf16[4,4,200,3,2,64]{2,5,4,3,1,0:T(8,128)(2,1)}, bf16[4,4,200,3,2,64]{2,5,4,1,3,0:T(8,128)(2,1)}, s32[4,4]{1,0:T(4,128)S(1)}, f32[4...) while((s32[]{:T(128)}, bf16[4,4,200,3,2,64]{2,5,4,3,1,0:T(8,128)(2,1)}, ...), condition=%wide.region_27.28_spmd, body=%wide.region_25.27_spmd.sunk | while | flops 208805600 | bytes 15790513 | solution.py:132
  525.3 4.6 copy.363
  529.9 4.6 all-to-all-start.7
  534.6 5.0 convolution_bitcast_fusion.4
  548.2 16.0 %all-to-all-done.7 = bf16[16,200,3,1,128]{4,1,3,2,0:T(8,128)(2,1)} async-done(((bf16[16,200,3,1,128]{4,1,3,2,0:T(8,128)(2,1)}), bf16[16,200,3,1,128]{4,1,3,2,0:T(8,128)(2,1)}, u32[]{:S(2)}, u32[]{:S(2)}) %all-to-all-start.7) | async-done | bytes 2457632 | tf_op jit(solution)/shard_map/all_to_all | solution.py:78
  564.1 4.7 copy.364
  571.9 3.4 copy.365
  575.3 4.5 reshape.604
  579.9 2.9 convolution_bitcast_fusion.5
  600.1 4.5 fusion.77
  607.9 41.2 %all-reduce = (f32[2,2,384]{2,1,0:T(2,128)S(1)}, f32[2,3840]{1,0:T(2,128)S(1)}) all-reduce(f32[2,2,384]{2,1,0:T(2,128)S(1)} %pad_maximum_fusion.26, f32[2,3840]{1,0:T(2,128)S(1)} %pad_maximum_fusion.22), channel_id=1, replica_groups=mesh['dp'=8,'tok'=4] {'dp','tok'}, use_global_device_ids=true, to_apply=%region_42.43 | all-reduce | flops 9216 | bytes 73728 | tf_op jit(solution)/shard_map/psum | solution.py:310
  650.4 2.8 multiply_add_fusion
  653.2 179.8 %all-reduce.4.cloned.1.call-done = (f32[2,384,1152]{2,1,0:T(8,128)}, f32[2,384,384]{2,1,0:T(8,128)}, f32[2,384,1536]{2,1,0:T(8,128)}, f32[2,1536,384]{2,1,0:T(8,128)}) async-done(((f32[2,384,1152]{2,1,0:T(8,128)}, f32[2,384,384]{2,1,0:T(8,128)}, f32[2,384,1536]{2,1,0:T(8,128)}, f32[2,1536,384]{2,1,0:T(8,128)}), (f32[2,384,1152]{2,1,0:T(8,128)}, f32[2,384,384]{2,1,0:T(8,128)}, f32[2,384,1536]{2,1,0:T(8,128)}, ...) | async-done | bytes 14155792 | tf_op jit(solution)/shard_map/psum | solution.py:310
  835.3 3.5 multiply_reduce_fusion.4
  848.4 3.4 subtract_bitcast_fusion.2
  853.7 3.6 subtract_bitcast_fusion
  859.6 2.8 subtract_bitcast_fusion.3
  863.3 3.1 subtract_bitcast_fusion.1
  877.9 12.1 %concatenate.67 = f32[443520]{0:T(1024)} concatenate(f32[110592]{0:T(1024)S(1)} %copy-done.47, f32[36864]{0:T(1024)S(1)} %copy-done.54, f32[147456]{0:T(1024)S(1)} %copy-done.42, f32[147456]{0:T(1024)S(1)} %copy-done.41, f32[192]{0:T(256)S(1)} %copy-done.92, f32[960]{0:T(1024)S(1)} %reshape.611), dimensions={0} | concatenate | bytes 3548160 | tf_op jit(solution)/shard_map/concatenate | solution.py:332
  (562 shorter events, 210.7 us)
Async XLA Ops:
  7.2 65.6 %copy-start.1 = (bf16[4,200,384]{2,1,0:T(8,128)(2,1)S(1)}, bf16[4,200,384]{2,1,0:T(8,128)(2,1)}, u32[]{:S(2)}) copy-start(bf16[4,200,384]{2,1,0:T(8,128)(2,1)} %param.23) | copy-start | bytes 1843204
  7.2 71.7 %all-gather.5.cloned.1.call-start = ((), (), s32[]{:S(2)}) async-start(), calls=%async_computation.8 | async-start | bytes 1990656 | tf_op jit(solution)/shard_map/all_gather | solution.py:171
  69.6 9.2 %copy-start.64 = (f32[1,3840]{1,0:T(1,128)}, f32[1,3840]{1,0:T(1,128)S(1)}, u32[]{:S(2)}) copy-start(f32[1,3840]{1,0:T(1,128)S(1)} %get-tuple-element.470) | copy-start | bytes 46084
  72.8 6.1 copy-start.62
  97.2 4.7 copy-start.43
  97.2 5.5 copy-start.107
  97.2 34.3 %all-to-all-start = ((bf16[4,200,3,4,128]{4,1,2,0,3:T(8,128)(2,1)}), bf16[4,200,3,4,128]{4,1,2,0,3:T(8,128)(2,1)}, u32[]{:S(2)}, u32[]{:S(2)}) async-start(bf16[4,200,3,4,128]{4,1,2,0,3:T(8,128)(2,1)} %copy.334), calls=%async_computation | async-start | bytes 4915200 | tf_op jit(solution)/shard_map/all_to_all | solution.py:57
  101.9 96.3 %all-gather.7.cloned.1.call-start = ((), (), s32[]{:S(2)}) async-start(), calls=%async_computation.9 | async-start | bytes 2654208 | tf_op jit(solution)/shard_map/all_gather | solution.py:173
  149.6 9.0 %copy-start = (bf16[4,4,200,3,2,64]{2,5,4,1,3,0:T(8,128)(2,1)}, bf16[4,4,200,3,2,64]{2,5,4,1,3,0:T(8,128)(2,1)S(1)}, u32[]{:S(2)}) copy-start(bf16[4,4,200,3,2,64]{2,5,4,1,3,0:T(8,128)(2,1)S(1)} %get-tuple-element.738) | copy-start | bytes 7372804
  152.5 41.4 %all-to-all-start.1 = ((bf16[16,200,1,128]{3,1,2,0:T(8,128)(2,1)}), bf16[16,200,1,128]{3,1,2,0:T(8,128)(2,1)}, u32[]{:S(2)}, u32[]{:S(2)}) async-start(bf16[16,200,1,128]{3,1,2,0:T(8,128)(2,1)} %copy.337), calls=%async_computation.1 | async-start | bytes 1638400 | tf_op jit(solution)/shard_map/all_to_all | solution.py:64
  156.7 58.0 %all-gather.9.cloned.1.call-start = ((), (), s32[]{:S(2)}) async-start(), calls=%async_computation.10 | async-start | bytes 2654208 | tf_op jit(solution)/shard_map/all_gather | solution.py:174
  160.9 37.4 %copy-start.83 = (f32[1536]{0:T(1024)}, f32[1536]{0:T(1024)S(1)}, u32[]{:S(2)}) copy-start(f32[1536]{0:T(1024)S(1)} %get-tuple-element.494) | copy-start | bytes 18436
  197.8 16.9 %copy-start.4 = (f32[800,384]{1,0:T(8,128)}, f32[800,384]{1,0:T(8,128)S(1)}, u32[]{:S(2)}) copy-start(f32[800,384]{1,0:T(8,128)S(1)} %get-tuple-element.476) | copy-start | bytes 3686404
  197.8 15.0 %copy-start.58 = (f32[800]{0:T(1024)}, f32[800]{0:T(1024)S(1)}, u32[]{:S(2)}) copy-start(f32[800]{0:T(1024)S(1)} %broadcast_multiply_fusion.10) | copy-start | bytes 9604
  198.2 14.7 %copy-start.60 = (f32[800]{0:T(1024)}, f32[800]{0:T(1024)S(1)}, u32[]{:S(2)}) copy-start(f32[800]{0:T(1024)S(1)} %add_rsqrt_fusion.2) | copy-start | bytes 9604
  198.3 16.4 %copy-start.106 = (f32[384]{0:T(512)S(1)}, f32[384]{0:T(512)}, u32[]{:S(2)}) copy-start(f32[384]{0:T(512)} %get-tuple-element.370) | copy-start | bytes 4612
  214.7 4.8 copy-start.77
  214.7 4.8 copy-start.89
  214.7 4.8 copy-start.104
  214.7 4.7 copy-start.113
  246.6 34.2 %all-to-all-start.2 = ((bf16[4,200,3,4,128]{4,1,2,0,3:T(8,128)(2,1)}), bf16[4,200,3,4,128]{4,1,2,0,3:T(8,128)(2,1)}, u32[]{:S(2)}, u32[]{:S(2)}) async-start(bf16[4,200,3,4,128]{4,1,2,0,3:T(8,128)(2,1)} %copy.342), calls=%async_computation.2 | async-start | bytes 4915200 | tf_op jit(solution)/shard_map/all_to_all | solution.py:57
  251.2 33.8 %copy-start.96 = (s32[4,4]{1,0:T(4,128)S(1)}, s32[4,4]{1,0:T(4,128)}, u32[]{:S(2)}) copy-start(s32[4,4]{1,0:T(4,128)} %get-tuple-element.772) | copy-start | bytes 196
  293.3 6.5 copy-start.108
  295.5 16.3 %all-to-all-start.3 = ((bf16[16,200,1,128]{3,1,2,0:T(8,128)(2,1)}), bf16[16,200,1,128]{3,1,2,0:T(8,128)(2,1)}, u32[]{:S(2)}, u32[]{:S(2)}) async-start(bf16[16,200,1,128]{3,1,2,0:T(8,128)(2,1)} %copy.345), calls=%async_computation.3 | async-start | bytes 1638400 | tf_op jit(solution)/shard_map/all_to_all | solution.py:64
  300.0 15.2 %copy-start.93 = (pred[800]{0:T(1024)(128)(4,1)}, pred[800]{0:T(1024)(128)(4,1)S(1)}, u32[]{:S(2)}) copy-start(pred[800]{0:T(1024)(128)(4,1)S(1)} %lt.134) | copy-start | bytes 2404
  323.0 19.7 %copy-start.6 = (f32[800,384]{1,0:T(8,128)}, f32[800,384]{1,0:T(8,128)S(1)}, u32[]{:S(2)}) copy-start(f32[800,384]{1,0:T(8,128)S(1)} %get-tuple-element.482) | copy-start | bytes 3686404
  323.4 12.8 %copy-start.53 = (bf16[4,200,384]{2,1,0:T(8,128)(2,1)S(1)}, bf16[4,200,384]{2,1,0:T(8,128)(2,1)}, u32[]{:S(2)}) copy-start(bf16[4,200,384]{2,1,0:T(8,128)(2,1)} %get-tuple-element.444) | copy-start | bytes 1843204
  323.4 12.8 %copy-start.109 = (bf16[2,1536,384]{2,1,0:T(8,128)(2,1)S(1)}, bf16[2,1536,384]{2,1,0:T(8,128)(2,1)}, u32[]{:S(2)}) copy-start(bf16[2,1536,384]{2,1,0:T(8,128)(2,1)} %all-gather.9.cloned.1.call-done) | copy-start | bytes 7077892
  358.5 16.3 %all-to-all-start.4 = ((bf16[4,200,4,128]{3,1,0,2:T(8,128)(2,1)}), bf16[4,200,4,128]{3,1,0,2:T(8,128)(2,1)}, u32[]{:S(2)}, u32[]{:S(2)}) async-start(bf16[4,200,4,128]{3,1,0,2:T(8,128)(2,1)} %copy.350), calls=%async_computation.4 | async-start | bytes 1638400 | tf_op jit(solution)/shard_map/all_to_all | solution.py:71
  407.2 4.7 copy-start.7
  407.2 34.3 %all-to-all-start.5 = ((bf16[16,200,3,1,128]{4,1,3,2,0:T(8,128)(2,1)}), bf16[16,200,3,1,128]{4,1,3,2,0:T(8,128)(2,1)}, u32[]{:S(2)}, u32[]{:S(2)}) async-start(bf16[16,200,3,1,128]{4,1,3,2,0:T(8,128)(2,1)} %copy.354), calls=%async_computation.5 | async-start | bytes 4915200 | tf_op jit(solution)/shard_map/all_to_all | solution.py:78
  452.7 5.5 copy-start.15
  463.5 8.6 copy-start.28
  464.0 5.9 copy-start.5
  464.0 5.9 copy-start.59
  464.0 5.9 copy-start.61
  464.0 5.9 copy-start.67
  464.0 5.9 copy-start.112
  482.5 16.3 %all-to-all-start.6 = ((bf16[4,200,4,128]{3,1,0,2:T(8,128)(2,1)}), bf16[4,200,4,128]{3,1,0,2:T(8,128)(2,1)}, u32[]{:S(2)}, u32[]{:S(2)}) async-start(bf16[4,200,4,128]{3,1,0,2:T(8,128)(2,1)} %copy.359), calls=%async_computation.6 | async-start | bytes 1638400 | tf_op jit(solution)/shard_map/all_to_all | solution.py:71
  486.7 5.1 copy-start.13
  486.7 5.1 copy-start.20
  529.9 4.7 copy-start.105
  529.9 34.3 %all-to-all-start.7 = ((bf16[16,200,3,1,128]{4,1,3,2,0:T(8,128)(2,1)}), bf16[16,200,3,1,128]{4,1,3,2,0:T(8,128)(2,1)}, u32[]{:S(2)}, u32[]{:S(2)}) async-start(bf16[16,200,3,1,128]{4,1,3,2,0:T(8,128)(2,1)} %copy.363), calls=%async_computation.7 | async-start | bytes 4915200 | tf_op jit(solution)/shard_map/all_to_all | solution.py:78
  534.5 298.5 %all-reduce.4.cloned.1.call-start = ((), (), s32[]{:S(2)}) async-start(), calls=%async_computation.11 | async-start | bytes 28311552 | tf_op jit(solution)/shard_map/psum | solution.py:310
  534.6 5.0 copy-start.29
  534.6 5.0 copy-start.115
  600.0 4.6 copy-start.102
  600.0 4.9 copy-start.76
  600.0 4.9 copy-start.100
  600.0 4.9 copy-start.78
  600.0 4.9 copy-start.87
  600.0 4.9 copy-start.99
  600.0 4.9 copy-start.98
  600.0 5.0 copy-start.24
  600.0 5.0 copy-start.74
  600.1 5.0 copy-start.114
  607.4 43.0 %copy-start.10 = (f32[800,384]{1,0:T(8,128)S(1)}, f32[800,384]{1,0:T(8,128)}, u32[]{:S(2)}) copy-start(f32[800,384]{1,0:T(8,128)} %copy-done.8) | copy-start | bytes 3686404
  833.0 5.8 copy-start.17
  841.2 5.7 copy-start.75
  841.2 5.7 copy-start.91
  841.2 5.9 copy-start.86
  841.2 5.9 copy-start.95
  848.4 5.3 copy-start.31
  848.4 5.3 copy-start.32
  (65 other events, 161.8 us)
Sparse Core Ops, SparseCore 0:
  10.9 50.0 all-gather.4
  105.5 51.8 all-gather.6
  160.3 54.3 all-gather.8
  585.1 247.8 all-reduce.3
where the time goes:
time: 911 us; the launch traced here: 898 us
  waiting for transfers between devices  305 us (33%)
  local copies, waits for them, and re-layouts  189 us (21%)
  blocking collectives  133 us (15%)
  matrix products  127 us (14%)
  other arithmetic  86.8 us (10%)
  starting transfers between devices  35.5 us (4%)
  between operations  20.9 us (2%)
    psum x1, waiting for transfers between devices, on_device(): lax.psum((grad_qkv_all, grad_proj_all, grad_fc1_all, grad_fc2_all, grad_g...  180 us
    all_to_all x2, waiting for transfers between devices, qkv_to_heads(): lax.all_to_all(sending, 'tok', split_axis=3, concat_axis=0, tiled=True)  57.7 us
    psum x1, blocking collectives, on_device(): lax.psum((grad_qkv_all, grad_proj_all, grad_fc1_all, grad_fc2_all, grad_g...  41.2 us
    all_to_all x2, waiting for transfers between devices, grads_to_rows(): lax.all_to_all(sending, 'tok', split_axis=0, concat_axis=3, tiled=True)  40.9 us
    all_gather x1, blocking collectives, on_device(): lax.all_gather(w_proj.astype(jnp.bfloat16), 'dp', axis=2, tiled=True)  33.1 us
    all_gather x1, blocking collectives, on_device(): lax.all_gather(norm_gains.astype(jnp.bfloat16), 'dp', axis=2, tiled=True)  31.1 us
    all_gather x1, blocking collectives, on_device(): lax.all_gather(biases.astype(jnp.bfloat16), 'dp', axis=1, tiled=True)  27.9 us
    dot_general x2, matrix products, on_device(): jnp.dot(a_second, up_weight, preferred_element_type=jnp.float32)  27.4 us
  transfers between devices with their start and end apart: 12, of which 9 were waited for; matrix products, arithmetic and copies ran while one was open for 12% of the time, Pallas kernels for 0%

commit v1 on v0

v1 whole, which is shorter than its diff:
```python
import functools
import math

import jax
import jax.numpy as jnp
from jax import lax
from jax.experimental import pallas as pl
from jax.experimental.pallas import tpu as pltpu
from jax.sharding import PartitionSpec as P

D = 384
HEADS = 6
HD = 64
FF = 1536
LAYERS = 2
STEP = 10
PAIRS = HEADS // 2
TILE = 128
EPS = 1e-06
HALF_ROOT = 0.7071067811865476
INV_ROOT_TAU = 0.3989422804014327
LOG2E = 1.4426950408889634
SCORE = 0.125 * LOG2E
TAIL_P = 0.4
TAIL = (
    0.22480539044849576,
    0.2382192213985389,
    0.13072083829499273,
    0.43284363894582684,
    -0.41172890451981375,
    0.7191256145749827,
    -0.41194367033429247,
    0.07795786677173361,
)
BF = jnp.bfloat16
F32 = jnp.float32


def nn(a, b):
    return lax.dot_general(a, b, (((1,), (0,)), ((), ())), preferred_element_type=F32)


def nt(a, b):
    return lax.dot_general(a, b, (((1,), (1,)), ((), ())), preferred_element_type=F32)


def tn(a, b):
    return lax.dot_general(a, b, (((0,), (0,)), ((), ())), preferred_element_type=F32)


def normalize(hidden):
    centered = hidden - jnp.mean(hidden, -1, keepdims=True)
    variance = jnp.mean(centered * centered, -1, keepdims=True)
    inverse = lax.rsqrt(variance + EPS)
    return centered * inverse, inverse


def norm_back(grad_n, normed, inverse):
    first = jnp.mean(grad_n, -1, keepdims=True)
    second = jnp.mean(grad_n * normed, -1, keepdims=True)
    return inverse * (grad_n - first - normed * second)


def gelu_pair(u):
    t = 1.0 / (1.0 + (TAIL_P * HALF_ROOT) * jnp.abs(u))
    bell = jnp.exp2(u * u * (-0.5 * LOG2E))
    poly = jnp.full_like(t, 0.5 * TAIL[-1])
    for coef in TAIL[-2::-1]:
        poly = poly * t + 0.5 * coef
    low = poly * t * bell
    cdf = jnp.where(u < 0.0, low, 1.0 - low)
    return u * cdf, cdf + u * bell * INV_ROOT_TAU


def rows_of(t):
    return pl.ds(pl.multiple_of(t * TILE, TILE), TILE)


def zero_tail(tiles, total, refs):
    def body(t, carry):
        for ref in refs:
            ref[rows_of(t), :] = jnp.zeros((TILE, ref.shape[1]), ref.dtype)
        return carry

    lax.fori_loop(tiles, total, body, 0)


def phase_qkv(tiles, h_ref, vec_ref, qkv_w, a_ref, qkv_ref):
    def body(t, carry):
        rows = rows_of(t)
        normed, _ = normalize(h_ref[rows, :])
        a = (normed * vec_ref[0:1, 0:D] + vec_ref[1:2, 0:D]).astype(BF)
        a_ref[rows, :] = a
        qkv_ref[rows, :] = (nt(a, qkv_w[...]) + vec_ref[7:8, 0 : 3 * D]).astype(BF)
        return carry

    lax.fori_loop(0, tiles, body, 0)


def head_mask(x, side):
    lane = lax.broadcasted_iota(jnp.int32, x.shape, 1)
    keep = (lane < HD) if side == 0 else (lane >= HD)
    return jnp.where(keep, x, jnp.zeros_like(x))


def pick(a, b):
    lane = lax.broadcasted_iota(jnp.int32, a.shape, 1)
    return jnp.where(lane < HD, a, b)


def attend(meta, seqs, slots, qkv_ref, o_ref, lse_ref):
    widths = window_sizes(slots)

    def seq_body(i, carry):
        length, start = meta[i], pl.multiple_of(meta[seqs + i], 16)

        def run(width):
            rows = pl.ds(start, width)
            for pair in range(PAIRS):
                at = pair * 2 * HD
                q = qkv_ref[rows, at : at + 2 * HD]
                k = qkv_ref[rows, D + at : D + at + 2 * HD]
                v = qkv_ref[rows, 2 * D + at : 2 * D + at + 2 * HD]
                outs = []
                for side in range(2):
                    s = nt(head_mask(k, side), q)
                    keep = lax.broadcasted_iota(jnp.int32, s.shape, 0) < length
                    s = jnp.where(keep, s, -1e30)
                    top = jnp.max(s, 0, keepdims=True)
                    e = jnp.exp2((s - top) * SCORE)
                    total = jnp.sum(e, 0, keepdims=True)
                    p = (e * (1.0 / total)).astype(BF)
                    outs.append(tn(p, v))
                    row = pair * 2 + side
                    lse_ref[i, row : row + 1, 0:width] = top * SCORE + jnp.log2(total)
                o_ref[rows, at : at + 2 * HD] = pick(*outs).astype(BF)

        low = 0
        for width in widths:
            pl.when(jnp.logical_and(length > low, length <= width))(functools.partial(run, width))
            low = width
        return carry

    lax.fori_loop(0, seqs, seq_body, 0)


def attend_back(meta, seqs, slots, qkv_ref, do_ref, lse_ref, dqkv_ref):
    widths = window_sizes(slots)

    def seq_body(i, carry):
        length, start = meta[i], pl.multiple_of(meta[seqs + i], 16)

        def run(width):
            rows = pl.ds(start, width)
            keep_rows = lax.broadcasted_iota(jnp.int32, (width, 2 * HD), 0) < length
            for pair in range(PAIRS):
                at = pair * 2 * HD
                q = qkv_ref[rows, at : at + 2 * HD]
                k = qkv_ref[rows, D + at : D + at + 2 * HD]
                v = qkv_ref[rows, 2 * D + at : 2 * D + at + 2 * HD]
                do = do_ref[rows, at : at + 2 * HD]
                do = jnp.where(keep_rows, do, jnp.zeros_like(do))
                dqs, dks, dvs = [], [], []
                for side in range(2):
                    s = nt(head_mask(k, side), q)
                    keep = lax.broadcasted_iota(jnp.int32, s.shape, 0) < length
                    row = pair * 2 + side
                    lse = lse_ref[i, row : row + 1, 0:width]
                    p = jnp.where(keep, jnp.exp2(s * SCORE - lse), 0.0)
                    dp = nt(head_mask(v, side), do)
                    inner = jnp.sum(p * dp, 0, keepdims=True)
                    ds = (p * (dp - inner)).astype(BF)
                    dvs.append(nn(p.astype(BF), do))
                    dks.append(nn(ds, q))
                    dqs.append(tn(ds, k))
                dqkv_ref[rows, at : at + 2 * HD] = (pick(*dqs) * 0.125).astype(BF)
                dqkv_ref[rows, D + at : D + at + 2 * HD] = (pick(*dks) * 0.125).astype(BF)
                dqkv_ref[rows, 2 * D + at : 2 * D + at + 2 * HD] = pick(*dvs).astype(BF)

        low = 0
        for width in widths:
            pl.when(jnp.logical_and(length > low, length <= width))(functools.partial(run, width))
            low = width
        return carry

    lax.fori_loop(0, seqs, seq_body, 0)


def window_sizes(slots):
    full = -(-slots // 16) * 16
    return [128, full] if full > 128 else [full]


def phase_mlp(tiles, h_ref, o_ref, vec_ref, proj_w, fc1_w, fc2_w, mid_ref, a_ref, act_ref, slope_ref, out_ref):
    def body(t, carry):
        rows = rows_of(t)
        mid = h_ref[rows, :] + nt(o_ref[rows, :], proj_w[...]) + vec_ref[4:5, 0:D]
        mid_ref[rows, :] = mid
        normed, _ = normalize(mid)
        a = (normed * vec_ref[2:3, 0:D] + vec_ref[3:4, 0:D]).astype(BF)
        a_ref[rows, :] = a
        for c in range(0, FF, 512):
            u = nt(a, fc1_w[c : c + 512, :]) + vec_ref[6:7, c : c + 512]
            act, slope = gelu_pair(u)
            act_ref[rows, c : c + 512] = act.astype(BF)
            slope_ref[rows, c : c + 512] = slope
        out_ref[rows, :] = mid + nn(act_ref[rows, :], fc2_w[...]) + vec_ref[5:6, 0:D]
        return carry

    lax.fori_loop(0, tiles, body, 0)


def add_row(ref, row, width, value):
    ref[row : row + 1, 0:width] += jnp.sum(value, 0, keepdims=True)


def phase_mlp_back(tiles, g_ref, mid_ref, slope_ref, vec_ref, fc1_w, fc2_w, proj_w, dm_ref, du_ref, g1_ref, dp_ref, do_ref, small_ref):
    def body(t, carry):
        rows = rows_of(t)
        g = g_ref[rows, :]
        dm = g.astype(BF)
        dm_ref[rows, :] = dm
        add_row(small_ref, 5, D, dm.astype(F32))
        for c in range(0, FF, 512):
            dact = nt(dm, fc2_w[c : c + 512, :])
            du = (dact * slope_ref[rows, c : c + 512]).astype(BF)
            du_ref[rows, c : c + 512] = du
            small_ref[6:7, c : c + 512] += jnp.sum(du.astype(F32), 0, keepdims=True)
        da = nn(du_ref[rows, :], fc1_w[...])
        normed, inverse = normalize(mid_ref[rows, :])
        add_row(small_ref, 2, D, da * normed)
        add_row(small_ref, 3, D, da)
        g1 = g + norm_back(da * vec_ref[2:3, 0:D], normed, inverse)
        g1_ref[rows, :] = g1
        dp = g1.astype(BF)
        dp_ref[rows, :] = dp
        add_row(small_ref, 4, D, dp.astype(F32))
        do_ref[rows, :] = nn(dp, proj_w[...]).astype(BF)
        return carry

    lax.fori_loop(0, tiles, body, 0)


def phase_qkv_back(tiles, h_ref, g1_ref, dqkv_ref, vec_ref, qkv_w, g_out, small_ref):
    def body(t, carry):
        rows = rows_of(t)
        dqkv = dqkv_ref[rows, :]
        add_row(small_ref, 7, 3 * D, dqkv.astype(F32))
        da = nn(dqkv, qkv_w[...])
        normed, inverse = normalize(h_ref[rows, :])
        add_row(small_ref, 0, D, da * normed)
        add_row(small_ref, 1, D, da)
        g_out[rows, :] = g1_ref[rows, :] + norm_back(da * vec_ref[0:1, 0:D], normed, inverse)
        return carry

    lax.fori_loop(0, tiles, body, 0)


def outer_products(tiles, total, jobs):
    half = -(-total // 2) * TILE
    rows = total * TILE
    step = 128
    for left, right, store in jobs:
        def body(m, carry, left=left, right=right, store=store):
            cols = pl.ds(pl.multiple_of(m * step, step), step)
            first = lambda: tn(left[0:half, cols], right[0:half, :])
            both = lambda: tn(left[0:rows, cols], right[0:rows, :])
            store(m * step, lax.cond(tiles * TILE > half, both, first))
            return carry

        lax.fori_loop(0, left.shape[1] // step, body, 0)


def store_rows(ref, base):
    def store(first, block):
        ref[pl.ds(pl.multiple_of(base + first, 128), 128), :] = block.astype(ref.dtype)

    return store


def vmem(n):
    return [pl.BlockSpec(memory_space=pltpu.VMEM)] * n


def call(body, name, outs, scratch, meta, *arrays):
    shapes = [jax.ShapeDtypeStruct(s, d) for s, d in outs]
    return pl.pallas_call(
        body,
        name=name,
        out_shape=shapes,
        in_specs=[pl.BlockSpec(memory_space=pltpu.SMEM)] + vmem(len(arrays)),
        out_specs=vmem(len(outs)),
        scratch_shapes=[pltpu.VMEM(s, d) for s, d in scratch],
        compiler_params=pltpu.CompilerParams(vmem_limit_bytes=56 << 20),
    )(meta, *arrays)


def plan_rows(lengths, slots):
    seqs = lengths.shape[0]
    room = (lengths + 15) // 16 * 16
    ends = jnp.cumsum(room)
    tiles = (ends[-1:] + TILE - 1) // TILE
    return jnp.concatenate([lengths, ends - room, tiles]).astype(jnp.int32)


def packed_tiles(seqs, slots):
    full = -(-slots // 16) * 16
    return -(-(seqs * full) // TILE)


def first_half(seqs, slots, total):
    rows = total * TILE

    def body(meta, x_ref, vec, qkv_w, h_ref, a_ref, qkv_ref, o_ref, lse_ref):
        tiles = meta[2 * seqs]
        h_ref[...] = jnp.zeros_like(h_ref)
        for i in range(seqs):
            at = pl.multiple_of(meta[seqs + i], 16)
            h_ref[pl.ds(at, slots), :] = x_ref[i].astype(F32)
        phase_qkv(tiles, h_ref, vec, qkv_w, a_ref, qkv_ref)
        zero_tail(tiles, total, [a_ref, qkv_ref])
        o_ref[...] = jnp.zeros_like(o_ref)
        attend(meta, seqs, slots, qkv_ref, o_ref, lse_ref)

    def run(meta, x, vec, qkv_w):
        outs = [((rows, D), F32), ((rows, D), BF), ((rows, 3 * D), BF), ((rows, D), BF), ((seqs, 8, 256), F32)]
        return call(body, "first_half", outs, [], meta, x, vec, qkv_w)

    return run


def middle(seqs, slots, total):
    rows = total * TILE

    def body(meta, h0, o0, vec0, proj_w, fc1_w, fc2_w, vec1, qkv_w, mid, a2, act, slope, h1, a1, qkv, o, lse):
        tiles = meta[2 * seqs]
        phase_mlp(tiles, h0, o0, vec0, proj_w, fc1_w, fc2_w, mid, a2, act, slope, h1)
        zero_tail(tiles, total, [a2, act])
        phase_qkv(tiles, h1, vec1, qkv_w, a1, qkv)
        zero_tail(tiles, total, [a1, qkv])
        o[...] = jnp.zeros_like(o)
        attend(meta, seqs, slots, qkv, o, lse)

    def run(meta, *args):
        outs = [
            ((rows, D), F32), ((rows, D), BF), ((rows, FF), BF), ((rows, FF), F32), ((rows, D), F32),
            ((rows, D), BF), ((rows, 3 * D), BF), ((rows, D), BF), ((seqs, 8, 256), F32),
        ]
        return call(body, "middle", outs, [], meta, *args)

    return run


def turn(seqs, slots, total):
    rows = total * TILE

    def body(meta, h, o, vec, proj_w, fc1_w, fc2_w, cot, out_ref, grads, small, g1, dp, do, mid, a2, act, slope, h2, dm, du):
        tiles = meta[2 * seqs]
        phase_mlp(tiles, h, o, vec, proj_w, fc1_w, fc2_w, mid, a2, act, slope, h2)
        for i in range(seqs):
            at = pl.multiple_of(meta[seqs + i], 16)
            keep = lax.broadcasted_iota(jnp.int32, (slots, D), 0) < meta[i]
            out_ref[i] = jnp.where(keep, h2[pl.ds(at, slots), :], 0.0).astype(out_ref.dtype)
        h2[...] = jnp.zeros_like(h2)
        for i in range(seqs):
            at = pl.multiple_of(meta[seqs + i], 16)
            keep = lax.broadcasted_iota(jnp.int32, (slots, D), 0) < meta[i]
            h2[pl.ds(at, slots), :] = jnp.where(keep, cot[i].astype(F32), 0.0)
        small[...] = jnp.zeros_like(small)
        phase_mlp_back(tiles, h2, mid, slope, vec, fc1_w, fc2_w, proj_w, dm, du, g1, dp, do, small)
        zero_tail(tiles, total, [a2, act, dm, du, dp, do])
        outer_products(tiles, total, [(du, a2, store_rows(grads, 0)), (act, dm, store_rows(grads, FF))])

    def run(meta, h, o, vec, proj_w, fc1_w, fc2_w, cot):
        outs = [
            (cot.shape, BF), ((2 * FF, D), BF), ((8, FF), F32), ((rows, D), F32), ((rows, D), BF), ((rows, D), BF),
        ]
        scratch = [
            ((rows, D), F32), ((rows, D), BF), ((rows, FF), BF), ((rows, FF), F32), ((rows, D), F32),
            ((rows, D), BF), ((rows, FF), BF),
        ]
        return call(body, "turn", outs, scratch, meta, h, o, vec, proj_w, fc1_w, fc2_w, cot)

    return run


def mlp_back(seqs, slots, total):
    rows = total * TILE

    def body(meta, g, mid, a2, act, slope, vec, fc1_w, fc2_w, proj_w, grads, small, g1, dp, do, dm, du):
        tiles = meta[2 * seqs]
        small[...] = jnp.zeros_like(small)
        phase_mlp_back(tiles, g, mid, slope, vec, fc1_w, fc2_w, proj_w, dm, du, g1, dp, do, small)
        zero_tail(tiles, total, [dm, du, dp, do])
        outer_products(tiles, total, [(du, a2, store_rows(grads, 0)), (act, dm, store_rows(grads, FF))])

    def run(meta, *args):
        outs = [((2 * FF, D), BF), ((8, FF), F32), ((rows, D), F32), ((rows, D), BF), ((rows, D), BF)]
        return call(body, "mlp_back", outs, [((rows, D), BF), ((rows, FF), BF)], meta, *args)

    return run


def attn_back(seqs, slots, total, last):
    rows = total * TILE

    def body(meta, h, qkv, lse, do, a1, o, dp, g1, vec, qkv_w, grads, small, g_out, dqkv, g_flat):
        tiles = meta[2 * seqs]
        small[...] = jnp.zeros_like(small)
        dqkv[...] = jnp.zeros_like(dqkv)
        attend_back(meta, seqs, slots, qkv, do, lse, dqkv)
        packed = g_flat if last else g_out
        phase_qkv_back(tiles, h, g1, dqkv, vec, qkv_w, packed, small)
        outer_products(tiles, total, [(dqkv, a1, store_rows(grads, 0)), (dp, o, store_rows(grads, 3 * D))])
        if last:
            for i in range(seqs):
                at = pl.multiple_of(meta[seqs + i], 16)
                keep = lax.broadcasted_iota(jnp.int32, (slots, D), 0) < meta[i]
                g_out[i] = jnp.where(keep, packed[pl.ds(at, slots), :], 0.0)

    def run(meta, *args):
        g_shape = (seqs, slots, D) if last else (rows, D)
        outs = [((4 * D, D), BF), ((8, FF), F32), (g_shape, F32)]
        flat = (rows, D) if last else (8, D)
        return call(body, "attn_back_last" if last else "attn_back", outs, [((rows, 3 * D), BF), (flat, F32)], meta, *args)

    return run


FAST = {"dp": 8, "tok": 4}
GATHER = (("dp", 2), ("dp", 4), ("dp", 1), ("tok", 2), ("tok", 1))


def swap(x, axis, bit):
    size = lax.axis_size(axis)
    return lax.ppermute(x, axis, [(i, i ^ bit) for i in range(size)])


def upper(axis, bit):
    return (lax.axis_index(axis) & bit) != 0


def gather_blocks(piece, steps=GATHER):
    cur = piece
    for axis, bit in steps:
        other = swap(cur, axis, bit)
        high = upper(axis, bit)
        cur = jnp.stack([jnp.where(high, other, cur), jnp.where(high, cur, other)])
    return cur


def scatter_blocks(blocks, steps=GATHER[::-1]):
    cur = blocks
    for axis, bit in steps:
        high = upper(axis, bit)
        mine = jnp.where(high, cur[1], cur[0]).astype(F32)
        away = jnp.where(high, cur[0], cur[1]).astype(BF)
        cur = mine + swap(away, axis, bit).astype(F32)
    return cur


def by_shard(full):
    full = full.transpose(0, 1, 3, 4, 2, 5, 6)
    return full.reshape(4, 8, full.shape[-2], D)


def from_shard(blocks):
    return blocks.reshape(2, 2, 2, 2, 2, blocks.shape[-2], D).transpose(0, 1, 4, 2, 3, 5, 6)


def own_quarter(shard):
    tok = lax.axis_index("tok")
    quarter = (tok % 2) * 2 + tok // 2
    rows = shard.shape[0] // 4
    return lax.dynamic_slice_in_dim(shard, quarter * rows, rows, 0)


def gather_fast(att, mlp):
    att_all = by_shard(gather_blocks(own_quarter(att)))
    mlp_all = by_shard(gather_blocks(own_quarter(mlp)))
    qkv = att_all[0:3].transpose(1, 0, 2, 3).reshape(3 * D, D)
    proj = att_all[3].reshape(D, D)
    up = mlp_all[0:2].transpose(1, 0, 2, 3).reshape(FF, D)
    down = mlp_all[2:4].transpose(1, 0, 2, 3).reshape(FF, D)
    return qkv, proj, up, down


def tok_gather(part):
    full = gather_blocks(part.astype(BF), GATHER[3:])
    return full.reshape(-1, D).astype(F32)


def scatter_mlp_fast(grads):
    up = grads[0:FF].reshape(8, 2, -1, D).transpose(1, 0, 2, 3)
    down = grads[FF:].reshape(8, 2, -1, D).transpose(1, 0, 2, 3)
    full = tok_gather(scatter_blocks(from_shard(jnp.concatenate([up, down]))))
    return full[0 : FF // 8], full[FF // 8 :]


def scatter_att_fast(grads):
    qkv = grads[0 : 3 * D].reshape(8, 3, -1, D).transpose(1, 0, 2, 3)
    proj = grads[3 * D :].reshape(1, 8, -1, D)
    full = tok_gather(scatter_blocks(from_shard(jnp.concatenate([qkv, proj]))))
    return full[0 : 3 * D // 8], full[3 * D // 8 :]


def gather_any(att, mlp):
    def whole(rows):
        return lax.all_gather(rows, "dp", axis=0, tiled=True)

    wide = att.shape[0] * 3 // 4
    half = mlp.shape[0] // 2
    return whole(att[:wide]), whole(att[wide:]), whole(mlp[:half]), whole(mlp[half:])


def scatter_any(grads, cut):
    def part(rows):
        return lax.psum(lax.psum_scatter(rows.astype(F32), "dp", scatter_dimension=0, tiled=True), "tok")

    return part(grads[:cut]), part(grads[cut:])


def sum_all_fast(x, steps):
    for axis, bit in steps:
        x = x + swap(x, axis, bit)
    return x


def adamw(weight, moments, clipped, rate, decay):
    first_mom = 0.9 * moments[0] + 0.1 * clipped
    second_mom = 0.999 * moments[1] + 0.001 * clipped * clipped
    fixed_first = first_mom / (1.0 - 0.9**STEP)
    fixed_second = second_mom / (1.0 - 0.999**STEP)
    new_weight = weight - rate * (fixed_first / (jnp.sqrt(fixed_second) + 1e-08) + decay * weight)
    return (jnp.stack([new_weight, first_mom]), second_mom)


def small_rows(gains, biases):
    gains, biases = gains.astype(F32), biases.astype(F32)

    def row(*parts):
        flat = jnp.concatenate(parts)
        return jnp.pad(flat, (0, FF - flat.shape[0]))

    cut = [biases[i * D : (i + 1) * D] for i in range(6)]
    qkv = row(cut[1], jnp.zeros((D,), F32), cut[2])
    return jnp.stack([row(gains[0]), row(cut[0]), row(gains[1]), row(cut[4]), row(cut[3]), row(cut[5]), biases[6 * D :], qkv])


def small_back(rows):
    gains = jnp.stack([rows[0, :D], rows[2, :D]])
    biases = jnp.concatenate([rows[1, :D], rows[7, :D], rows[7, 2 * D : 3 * D], rows[4, :D], rows[3, :D], rows[5, :D], rows[6]])
    return gains, biases


def on_device(x, cot, lengths, w_qkv, w_proj, w_fc1, w_fc2, norm_gains, biases,
              mom_qkv, mom_proj, mom_fc1, mom_fc2, mom_gains, mom_biases):
    fast = all(lax.axis_size(a) == n for a, n in FAST.items())
    seqs, slots = x.shape[0], x.shape[1]
    own = lax.dynamic_slice_in_dim(lengths, lax.axis_index("tok") * seqs, seqs, 0)
    meta = plan_rows(own, slots)
    total = packed_tiles(seqs, slots)
    size = (seqs, slots, total)
    att = [jnp.concatenate([w_qkv[l].T, w_proj[l].T]).astype(BF) for l in range(LAYERS)]
    mlp = [jnp.concatenate([w_fc1[l].T, w_fc2[l]]).astype(BF) for l in range(LAYERS)]
    small = jnp.concatenate([norm_gains.reshape(LAYERS, -1), biases], 1).astype(BF)
    gather = gather_fast if fast else gather_any
    if fast:
        small = gather_blocks(small, GATHER[:3]).transpose(1, 2, 0, 3, 4).reshape(-1, *small.shape)
    else:
        small = lax.all_gather(small, "dp")
    shards = small.shape[0]
    cut = 2 * D // shards
    gains_all = small[:, :, :cut].reshape(shards, LAYERS, 2, -1).transpose(1, 2, 0, 3).reshape(LAYERS, 2, D)
    biases_all = small[:, :, cut:].transpose(1, 0, 2).reshape(LAYERS, -1)
    vecs = [small_rows(gains_all[l], biases_all[l]) for l in range(LAYERS)]
    qkv0, proj0, up0, down0 = gather(att[0], mlp[0])
    qkv1, proj1, up1, down1 = gather(att[1], mlp[1])
    h0, a0, p0, o0, lse0 = first_half(*size)(meta, x, vecs[0], qkv0)
    mid0, b0, act0, slope0, h1, a1, p1, o1, lse1 = middle(*size)(
        meta, h0, o0, vecs[0], proj0, up0, down0, vecs[1], qkv1
    )
    layer_out, mlp1, small1a, g1, dp1, do1 = turn(*size)(meta, h1, o1, vecs[1], proj1, up1, down1, cot)
    scatter_mlp = scatter_mlp_fast if fast else (lambda g: scatter_any(g, FF))
    scatter_att = scatter_att_fast if fast else (lambda g: scatter_any(g, 3 * D))
    att1, small1b, g = attn_back(*size, False)(meta, h1, p1, lse1, do1, a1, o1, dp1, g1, vecs[1], qkv1)
    mlp0, small0a, g1, dp0, do0 = mlp_back(*size)(meta, g, mid0, b0, act0, slope0, vecs[0], up0, down0, proj0)
    att0, small0b, input_grad = attn_back(*size, True)(
        meta, h0, p0, lse0, do0, a0, o0, dp0, g1, vecs[0], qkv0
    )
    up_g1, down_g1 = scatter_mlp(mlp1)
    qkv_g1, proj_g1 = scatter_att(att1)
    up_g0, down_g0 = scatter_mlp(mlp0)
    qkv_g0, proj_g0 = scatter_att(att0)
    smalls = jnp.stack([small0a + small0b, small1a + small1b])
    smalls = sum_all_fast(smalls, GATHER) if fast else lax.psum(smalls, ("dp", "tok"))
    grads = [
        jnp.stack([qkv_g0.T, qkv_g1.T]),
        jnp.stack([proj_g0.T, proj_g1.T]),
        jnp.stack([up_g0.T, up_g1.T]),
        jnp.stack([down_g0, down_g1]),
    ]
    gains_g, biases_g = (jnp.stack(t) for t in zip(*(small_back(smalls[l]) for l in range(LAYERS))))
    squares = sum(jnp.sum(g * g) for g in grads)
    squares = sum_all_fast(squares, GATHER[:3]) if fast else lax.psum(squares, "dp")
    squares = squares + jnp.sum(gains_g * gains_g) + jnp.sum(biases_g * biases_g)
    dp_index = lax.axis_index("dp")
    grads.append(lax.dynamic_slice_in_dim(gains_g, dp_index * norm_gains.shape[2], norm_gains.shape[2], 2))
    grads.append(lax.dynamic_slice_in_dim(biases_g, dp_index * biases.shape[1], biases.shape[1], 1))
    grad_norm = jnp.sqrt(squares)
    limit = 0.25 * math.sqrt(LAYERS * (4 * D * D + 2 * D * FF + 8 * D + FF))
    factor = jnp.minimum(1.0, limit / (grad_norm + 1e-06))
    masters = (w_qkv, w_proj, w_fc1, w_fc2, norm_gains, biases)
    moments = (mom_qkv, mom_proj, mom_fc1, mom_fc2, mom_gains, mom_biases)
    states, seconds = [], []
    for index in range(6):
        rate, decay = (0.08, 0.05) if index < 4 else (0.4, 0.0)
        state, second = adamw(masters[index], moments[index], grads[index] * factor, rate, decay)
        states.append(state)
        seconds.append(second.reshape(-1))
    return (layer_out, input_grad, grad_norm, *states, jnp.concatenate(seconds))


def solution(mesh):
    rows = P(("dp", "tok"), None, None)
    weights = (P(None, None, "dp"),) * 3 + (P(None, "dp", None), P(None, None, "dp"), P(None, "dp"))
    stacked = tuple(P(None, *spec) for spec in weights)
    return jax.shard_map(
        on_device,
        mesh=mesh,
        in_specs=(rows, rows, P("dp"), *weights, *stacked),
        out_specs=(rows, rows, P(), *stacked, P("dp")),
        check_vma=False,
    )
```

time: 911 us -> 410 us (0.45); the launches traced: 898 us -> 407 us
  waiting for transfers between devices: 305 us -> 116 us
  local copies, waits for them, and re-layouts: 189 us -> 50.5 us
  Pallas kernels: 0 us -> 133 us
  blocking collectives: 133 us -> 0 us
  matrix products: 127 us -> 0 us
  other arithmetic: 86.8 us -> 32.8 us
  starting transfers between devices: 35.5 us -> 65.4 us
  between operations: 20.9 us -> 10.5 us
    psum x1 -> x0, waiting for transfers between devices: 180 us -> none  [on_device(): lax.psum((grad_qkv_all, grad_proj_all, grad_fc1_all, grad_fc2_all, grad_g...]
    pallas_call x0 -> x6, Pallas kernels: none -> 133 us  [call(): pl.pallas_call(body, name=name, out_shape=shapes, in_specs=[pl.BlockSpec(...]
    dot_general x80 -> x0, matrix products: 127 us -> none  [the longest x2 27.4 us: on_device(): jnp.dot(a_second, up_weight, preferred_element_type=jnp.float32)]
    all_to_all x8 -> x0, waiting for transfers between devices: 124 us -> none  [the longest x2 57.7 us: qkv_to_heads(): lax.all_to_all(sending, 'tok', split_axis=3, concat_axis=0, tiled=True)]
    ppermute x0 -> x59, waiting for transfers between devices: none -> 116 us  [swap(): return lax.ppermute(x, axis, [(i, i ^ bit) for i in range(size)])]
    all_gather x3 -> x0, blocking collectives: 92 us -> none  [the longest x1 33.1 us: on_device(): lax.all_gather(w_proj.astype(jnp.bfloat16), 'dp', axis=2, tiled=True)]
    ppermute x0 -> x59, starting transfers between devices: none -> 65.4 us  [swap(): return lax.ppermute(x, axis, [(i, i ^ bit) for i in range(size)])]
    reshape x19 -> x8, local copies, waits for them, and re-layouts: 59.7 us -> 1.37 us  [the longest x4 1.04 us: from_shard(): blocks.reshape(2, 2, 2, 2, 2, blocks.shape[-2], D)]
  transfers between devices with their start and end apart: 12 -> 59, of which waited for: 9 -> 36; matrix products, arithmetic and copies ran while one was open for 12% -> 7% of each run, Pallas kernels for 0% -> 3%
where the time goes in v1:
time: 410 us; the launch traced here: 407 us
  Pallas kernels  133 us (32%)
  waiting for transfers between devices  116 us (28%)
  starting transfers between devices  65.4 us (16%)
  local copies, waits for them, and re-layouts  50.5 us (12%)
  other arithmetic  32.8 us (8%)
  between operations  10.5 us (3%)
    pallas_call x6, Pallas kernels, call(): pl.pallas_call(body, name=name, out_shape=shapes, in_specs=[pl.BlockSpec(...  133 us
    ppermute x59, waiting for transfers between devices, swap(): return lax.ppermute(x, axis, [(i, i ^ bit) for i in range(size)])  116 us
    ppermute x59, starting transfers between devices, swap(): return lax.ppermute(x, axis, [(i, i ^ bit) for i in range(size)])  65.4 us
    concatenate x1, local copies, waits for them, and re-layouts, on_device(): return (layer_out, input_grad, grad_norm, *states, jnp.concatenate(seconds))  12 us
    another operation x14, other arithmetic, adamw(): return (jnp.stack([new_weight, first_mom]), second_mom)  11.2 us
  transfers between devices with their start and end apart: 59, of which 36 were waited for; matrix products, arithmetic and copies ran while one was open for 7% of the time, Pallas kernels for 3%

profile of v1, /device:TPU:0, one launch (start us, length us, event | category | flops | bytes accessed | tf_op | source)
XLA Modules:
  0.0 407.4 jit_solution(4799069038642660933)
XLA Ops:
  2.1 3.1 collective-permute-start.18
  6.2 1.5 collective-permute-start.8
  8.6 1.4 collective-permute-start
  10.3 1.9 collective-permute-done
  12.3 2.7 collective-permute-start.1
  17.0 1.6 collective-permute-start.2
  19.1 1.6 collective-permute-done.2
  23.4 2.7 collective-permute-start.14
  26.6 2.7 collective-permute-start.19
  29.7 6.9 %collective-permute-done.14 = bf16[2,48,384]{2,1,0:T(8,128)(2,1)S(1)} collective-permute-done((bf16[2,48,384]{2,1,0:T(8,128)(2,1)S(1)}, bf16[2,48,384]{2,1,0:T(8,128)(2,1)S(1)}, u32[]{:S(2)}, u32[]{:S(2)}) %collective-permute-start.14) | collective-permute-done | bytes 73760 | tf_op jit(solution)/shard_map/ppermute | solution.py:436
  36.6 1.6 collective-permute-start.15
  38.2 1.5 collective-permute-start.5
  39.8 1.5 collective-permute-done.19
  41.4 1.6 collective-permute-start.20
  43.1 1.5 collective-permute-start.10
  44.7 1.6 collective-permute-start.16
  47.4 4.6 %collective-permute-done.20 = bf16[2,2,96,384]{3,2,1,0:T(8,128)(2,1)S(1)} collective-permute-done((bf16[2,2,96,384]{3,2,1,0:T(8,128)(2,1)S(1)}, bf16[2,2,96,384]{3,2,1,0:T(8,128)(2,1)S(1)}, u32[]{:S(2)}, u32[]{:S(2)}) %collective-permute-start.20) | collective-permute-done | bytes 294944 | tf_op jit(solution)/shard_map/ppermute | solution.py:436
  52.2 1.6 collective-permute-start.21
  53.8 2.3 collective-permute-done.10
  56.2 1.6 collective-permute-start.11
  58.0 3.0 collective-permute-done.6
  61.3 12.4 %collective-permute-done.21 = bf16[2,2,2,96,384]{4,3,2,1,0:T(8,128)(2,1)S(1)} collective-permute-done((bf16[2,2,2,96,384]{4,3,2,1,0:T(8,128)(2,1)S(1)}, bf16[2,2,2,96,384]{4,3,2,1,0:T(8,128)(2,1)S(1)}, u32[]{:S(2)}, u32[]{:S(2)}) %collective-permute-start.21) | collective-permute-done | bytes 589856 | tf_op jit(solution)/shard_map/ppermute | solution.py:436
  74.0 9.5 %collective-permute-done.11 = bf16[2,2,2,96,384]{4,3,0,2,1:T(8,128)(2,1)S(1)} collective-permute-done((bf16[2,2,2,96,384]{4,3,0,2,1:T(8,128)(2,1)S(1)}, bf16[2,2,2,96,384]{4,3,0,2,1:T(8,128)(2,1)S(1)}, u32[]{:S(2)}, u32[]{:S(2)}) %collective-permute-start.11) | collective-permute-done | bytes 589856 | tf_op jit(solution)/shard_map/ppermute | solution.py:436
  88.3 11.8 %first_half.1 = (f32[896,384]{1,0:T(8,128)}, bf16[896,384]{1,0:T(8,128)(2,1)}, bf16[896,1152]{1,0:T(8,128)(2,1)}, bf16[896,384]{1,0:T(8,128)(2,1)}, f32[4,8,256]{2,1,0:T(8,128)}) custom-call(s32[9]{0:T(128)} %pad_add_fusion.meta, bf16[4,200,384]{2,1,0:T(8,128)(2,1)} %x_ref.1, f32[8,1536]{1,0:T(8,128)} %stack.489.vec.vec0, bf16[1152,384]{1,0:T(8,128)(2,1)} %bitcast.500), custom_call_target="tpu_custom_call" | custom-call | tf_op jit(solution)/shard_map/first_half/pallas_call | solution.py:287
  106.8 24.6 %middle.1 = (f32[896,384]{1,0:T(8,128)}, bf16[896,384]{1,0:T(8,128)(2,1)}, bf16[896,1536]{1,0:T(8,128)(2,1)}, f32[896,1536]{1,0:T(8,128)}, f32[896,384]{1,0:T(8,...) custom-call(s32[9]{0:T(128)} %pad_add_fusion.meta, ...), custom_call_target="tpu_custom_call" | custom-call | tf_op jit(solution)/shard_map/middle/pallas_call | solution.py:287
  131.4 27.6 %turn.1 = (bf16[4,200,384]{2,1,0:T(8,128)(2,1)}, bf16[3072,384]{1,0:T(8,128)(2,1)}, f32[8,1536]{1,0:T(8,128)}, f32[896,384]{1,0:T(8,128)}, bf16[896,384]{1,0:T(8,128)(2,1)}, /*index=5*/bf16[896,384]{1,0:T(8,128)(2,1)}) custom-call(s32[9]{0:T(128)} %pad_add_fusion.meta, f32[896,384]{1,0:T(8,128)} %get-tuple-element.43.h, ...), custom_call_target="tpu_custom_call" | custom-call | tf_op jit(solution)/shard_map/turn/pallas_call | solution.py:287
  158.9 19.3 %attn_back.1 = (bf16[1536,384]{1,0:T(8,128)(2,1)}, f32[8,1536]{1,0:T(8,128)}, f32[896,384]{1,0:T(8,128)}) custom-call(s32[9]{0:T(128)} %pad_add_fusion.meta, f32[896,384]{1,0:T(8,128)} %get-tuple-element.43.h, bf16[896,1152]{1,0:T(8,128)(2,1)} %get-tuple-element.48.qkv, f32[4,8,256]{2,1,0:T(8,128)} %get-tuple-element.49.lse, ...), custom_call_target="tpu_custom_call" | custom-call | tf_op jit(solution)/shard_map/attn_back/pallas_call | solution.py:287
  178.3 21.1 %mlp_back.1 = (bf16[3072,384]{1,0:T(8,128)(2,1)}, f32[8,1536]{1,0:T(8,128)}, f32[896,384]{1,0:T(8,128)}, bf16[896,384]{1,0:T(8,128)(2,1)}, bf16[896,384]{1,0:T(8,128)(2,1)}) custom-call(s32[9]{0:T(128)} %pad_add_fusion.meta, f32[896,384]{1,0:T(8,128)} %get-tuple-element.54.g, f32[896,384]{1,0:T(8,128)} %get-tuple-element.55.mid, ...), custom_call_target="tpu_custom_call" | custom-call | tf_op jit(solution)/shard_map/mlp_back/pallas_call | solution.py:287
  199.4 28.1 %attn_back_last.1 = (bf16[1536,384]{1,0:T(8,128)(2,1)}, f32[8,1536]{1,0:T(8,128)}, f32[4,200,384]{2,1,0:T(8,128)}) custom-call(s32[9]{0:T(128)} %pad_add_fusion.meta, f32[896,384]{1,0:T(8,128)} %get-tuple-element.41.h0.h, bf16[896,1152]{1,0:T(8,128)(2,1)} %get-tuple-element.46.qkv, f32[4,8,256]{2,1,0:T(8,128)} %get-tuple-element.47.lse, ...), custom_call_target="tpu_custom_call" | custom-call | tf_op jit(solution)/shard_map/attn_back_last/pallas_call | solution.py:287
  227.5 1.4 slice.515
  232.7 1.4 copy-done.6
  235.4 6.7 %collective-permute-start.55 = (f32[2,8,1536]{2,1,0:T(8,128)S(1)}, f32[2,8,1536]{2,1,0:T(8,128)S(1)}, u32[]{:S(2)}, u32[]{:S(2)}) collective-permute-start(f32[2,8,1536]{2,1,0:T(8,128)S(1)} %fusion.91), channel_id=1, source_target_pairs={{0,16},{4,20},{8,24},{12,28},{16,0},{20,4},{24,8},{28,12},{1,17},{... | collective-permute-start | bytes 294920 | tf_op jit(solution)/shard_map/ppermute | solution.py:436
  242.4 4.8 %collective-permute-done.55 = f32[2,8,1536]{2,1,0:T(8,128)S(1)} collective-permute-done((f32[2,8,1536]{2,1,0:T(8,128)S(1)}, f32[2,8,1536]{2,1,0:T(8,128)S(1)}, u32[]{:S(2)}, u32[]{:S(2)}) %collective-permute-start.55) | collective-permute-done | bytes 98336 | tf_op jit(solution)/shard_map/ppermute | solution.py:436
  247.4 4.4 %collective-permute-done.56 = f32[2,8,1536]{2,1,0:T(8,128)S(1)} collective-permute-done((f32[2,8,1536]{2,1,0:T(8,128)S(1)}, f32[2,8,1536]{2,1,0:T(8,128)S(1)}, u32[]{:S(2)}, u32[]{:S(2)}) %collective-permute-start.56) | collective-permute-done | bytes 98336 | tf_op jit(solution)/shard_map/ppermute | solution.py:436
  252.3 4.3 %collective-permute-done.57 = f32[2,8,1536]{2,1,0:T(8,128)S(1)} collective-permute-done((f32[2,8,1536]{2,1,0:T(8,128)S(1)}, f32[2,8,1536]{2,1,0:T(8,128)S(1)}, u32[]{:S(2)}, u32[]{:S(2)}) %collective-permute-start.57) | collective-permute-done | bytes 98336 | tf_op jit(solution)/shard_map/ppermute | solution.py:436
  260.4 2.1 collective-permute-start.31
  262.5 7.5 %collective-permute-done.24 = bf16[2,2,2,48,384]{4,3,2,1,0:T(8,128)(2,1)S(1)} collective-permute-done((bf16[2,2,2,48,384]{4,3,2,1,0:T(8,128)(2,1)S(1)}, bf16[2,2,2,48,384]{4,3,2,1,0:T(8,128)(2,1)S(1)}, u32[]{:S(2)}, u32[]{:S(2)}) %collective-permute-start.24) | collective-permute-done | bytes 294944 | tf_op jit(solution)/shard_map/ppermute | solution.py:436
  270.2 5.3 %collective-permute-done.31 = bf16[2,2,2,48,384]{4,3,2,1,0:T(8,128)(2,1)S(1)} collective-permute-done((bf16[2,2,2,48,384]{4,3,2,1,0:T(8,128)(2,1)S(1)}, bf16[2,2,2,48,384]{4,3,2,1,0:T(8,128)(2,1)S(1)}, u32[]{:S(2)}, u32[]{:S(2)}) %collective-permute-start.31) | collective-permute-done | bytes 294944 | tf_op jit(solution)/shard_map/ppermute | solution.py:436
  276.5 4.3 %collective-permute-done.32 = bf16[2,2,48,384]{3,2,1,0:T(8,128)(2,1)S(1)} collective-permute-done((bf16[2,2,48,384]{3,2,1,0:T(8,128)(2,1)S(1)}, bf16[2,2,48,384]{3,2,1,0:T(8,128)(2,1)S(1)}, u32[]{:S(2)}, u32[]{:S(2)}) %collective-permute-start.32) | collective-permute-done | bytes 147488 | tf_op jit(solution)/shard_map/ppermute | solution.py:436
  282.0 2.7 collective-permute-start.27
  284.6 2.5 collective-permute-done.33
  287.9 3.3 collective-permute-done.34
  293.1 1.5 collective-permute-start.38
  303.8 5.8 %collective-permute-done.38 = bf16[2,2,2,96,384]{4,3,2,1,0:T(8,128)(2,1)S(1)} collective-permute-done((bf16[2,2,2,96,384]{4,3,2,1,0:T(8,128)(2,1)}, bf16[2,2,2,96,384]{4,3,2,1,0:T(8,128)(2,1)S(1)}, u32[]{:S(2)}, u32[]{:S(2)}) %collective-permute-start.38) | collective-permute-done | bytes 589856 | tf_op jit(solution)/shard_map/ppermute | solution.py:436
  310.1 7.6 %collective-permute-done.45 = bf16[2,2,2,96,384]{4,3,2,1,0:T(8,128)(2,1)S(1)} collective-permute-done((bf16[2,2,2,96,384]{4,3,2,1,0:T(8,128)(2,1)}, bf16[2,2,2,96,384]{4,3,2,1,0:T(8,128)(2,1)S(1)}, u32[]{:S(2)}, u32[]{:S(2)}) %collective-permute-start.45) | collective-permute-done | bytes 589856 | tf_op jit(solution)/shard_map/ppermute | solution.py:436
  319.1 1.5 collective-permute-start.40
  320.6 4.1 %collective-permute-done.46 = bf16[2,2,96,384]{3,2,1,0:T(8,128)(2,1)S(1)} collective-permute-done((bf16[2,2,96,384]{3,2,1,0:T(8,128)(2,1)S(1)}, bf16[2,2,96,384]{3,2,1,0:T(8,128)(2,1)S(1)}, u32[]{:S(2)}, u32[]{:S(2)}) %collective-permute-start.46) | collective-permute-done | bytes 294944 | tf_op jit(solution)/shard_map/ppermute | solution.py:436
  324.9 1.6 collective-permute-start.47
  326.5 3.2 collective-permute-done.40
  329.7 1.5 collective-permute-start.41
  331.2 1.7 collective-permute-done.47
  333.0 1.4 collective-permute-done.41
  334.4 2.9 collective-permute-start.42
  337.4 1.5 collective-permute-start.49
  339.7 2.0 collective-permute-done.49
  346.3 1.4 collective-permute-start.51
  347.6 2.3 collective-permute-done.51
  350.6 3.0 collective-permute-start.52
  353.6 1.6 collective-permute-done.52
  355.8 2.5 collective-permute-start.53
  365.3 2.5 subtract_bitcast_fusion.1
  367.9 1.5 copy.62
  374.5 1.8 slice_multiply_fusion.6
  394.0 12.0 %concatenate.92 = f32[443520]{0:T(1024)} concatenate(f32[110592]{0:T(1024)S(1)} %fusion.30, f32[36864]{0:T(1024)S(1)} %fusion.45, f32[147456]{0:T(1024)S(1)} %fusion.12, f32[147456]{0:T(1024)S(1)} %fusion.13, f32[192]{0:T(256)S(1)} %reshape.478, f32[960]{0:T(1024)S(1)} %reshape.479), dimensions={0} | concatenate | bytes 3548160 | tf_op jit(solution)/shard_map/concatenate | solution.py:621
  (460 shorter events, 78.6 us)
Async XLA Ops:
  2.1 7.9 %copy-start.57 = (s32[16]{0:T(128)S(1)}, s32[16]{0:T(128)}, u32[]{:S(2)}) copy-start(s32[16]{0:T(128)} %param.17) | copy-start | bytes 196
  2.1 24.4 %collective-permute-start.18 = (bf16[96,384]{1,0:T(8,128)(2,1)S(1)}, bf16[96,384]{1,0:T(8,128)(2,1)S(1)}, u32[]{:S(2)}, u32[]{:S(2)}) collective-permute-start(bf16[96,384]{1,0:T(8,128)(2,1)S(1)} %fusion.60), channel_id=1, source_target_pairs={{0,8},{4,12},{8,0},{12,4},{16,24},{20,28},{24,16},{28,20},{1,9},{5... | collective-permute-start | bytes 221192 | tf_op jit(solution)/shard_map/ppermute | solution.py:436
  5.3 15.9 %copy-start.56 = (pred[1536]{0:T(1024)(128)(4,1)S(1)}, pred[1536]{0:T(1024)(128)(4,1)}, u32[]{:S(2)}) copy-start(pred[1536]{0:T(1024)(128)(4,1)} %constant.176.clone.1) | copy-start | bytes 4612
  5.4 18.0 %collective-permute-start.13 = (bf16[48,384]{1,0:T(8,128)(2,1)S(1)}, bf16[48,384]{1,0:T(8,128)(2,1)S(1)}, u32[]{:S(2)}, u32[]{:S(2)}) collective-permute-start(bf16[48,384]{1,0:T(8,128)(2,1)S(1)} %fusion.66), channel_id=1, source_target_pairs={{0,8},{4,12},{8,0},{12,4},{16,24},{20,28},{24,16},{28,20},{1,9},{5... | collective-permute-start | bytes 110600 | tf_op jit(solution)/shard_map/ppermute | solution.py:436
  6.2 23.0 %collective-permute-start.8 = (bf16[96,384]{1,0:T(8,128)(2,1)S(1)}, bf16[96,384]{1,0:T(8,128)(2,1)S(1)}, u32[]{:S(2)}, u32[]{:S(2)}) collective-permute-start(bf16[96,384]{1,0:T(8,128)(2,1)S(1)} %fusion.61), channel_id=1, source_target_pairs={{0,8},{4,12},{8,0},{12,4},{16,24},{20,28},{24,16},{28,20},{1,9},{5... | collective-permute-start | bytes 221192 | tf_op jit(solution)/shard_map/ppermute | solution.py:436
  7.7 18.4 %collective-permute-start.3 = (bf16[48,384]{1,0:T(8,128)(2,1)S(1)}, bf16[48,384]{1,0:T(8,128)(2,1)S(1)}, u32[]{:S(2)}, u32[]{:S(2)}) collective-permute-start(bf16[48,384]{1,0:T(8,128)(2,1)S(1)} %fusion.67), channel_id=1, source_target_pairs={{0,8},{4,12},{8,0},{12,4},{16,24},{20,28},{24,16},{28,20},{1,9},{5... | collective-permute-start | bytes 110600 | tf_op jit(solution)/shard_map/ppermute | solution.py:436
  8.6 3.6 collective-permute-start
  12.3 4.6 %collective-permute-start.1 = (bf16[2,2,576]{2,1,0:T(2,128)(2,1)S(1)}, bf16[2,2,576]{2,1,0:T(2,128)(2,1)S(1)}, u32[]{:S(2)}, u32[]{:S(2)}) collective-permute-start(bf16[2,2,576]{2,1,0:T(2,128)(2,1)S(1)} %pad_maximum_fusion.42), channel_id=1, source_target_pairs={{0,16},{4,20},{8,24},{12,28},{16,0},{20,4},{24,8},{28,12},{1,17},{... | collective-permute-start | bytes 13832 | tf_op jit(solution)/shard_map/ppermute | solution.py:436
  17.0 3.7 collective-permute-start.2
  23.4 13.1 %collective-permute-start.14 = (bf16[2,48,384]{2,1,0:T(8,128)(2,1)S(1)}, bf16[2,48,384]{2,1,0:T(8,128)(2,1)S(1)}, u32[]{:S(2)}, u32[]{:S(2)}) collective-permute-start(bf16[2,48,384]{2,1,0:T(8,128)(2,1)S(1)} %pad_maximum_fusion.33), channel_id=1, source_target_pairs={{0,16},{4,20},{8,24},{12,28},{16,0},{20,4},{24,8},{28,12},{1,17},{... | collective-permute-start | bytes 221192 | tf_op jit(solution)/shard_map/ppermute | solution.py:436
  26.1 12.1 %collective-permute-start.4 = (bf16[2,48,384]{2,1,0:T(8,128)(2,1)S(1)}, bf16[2,48,384]{2,1,0:T(8,128)(2,1)S(1)}, u32[]{:S(2)}, u32[]{:S(2)}) collective-permute-start(bf16[2,48,384]{2,1,0:T(8,128)(2,1)S(1)} %pad_maximum_fusion.32), channel_id=1, source_target_pairs={{0,16},{4,20},{8,24},{12,28},{16,0},{20,4},{24,8},{28,12},{1,17},{... | collective-permute-start | bytes 221192 | tf_op jit(solution)/shard_map/ppermute | solution.py:436
  26.6 14.7 %collective-permute-start.19 = (bf16[2,96,384]{2,1,0:T(8,128)(2,1)S(1)}, bf16[2,96,384]{2,1,0:T(8,128)(2,1)S(1)}, u32[]{:S(2)}, u32[]{:S(2)}) collective-permute-start(bf16[2,96,384]{2,1,0:T(8,128)(2,1)S(1)} %pad_maximum_fusion.25), channel_id=1, source_target_pairs={{0,16},{4,20},{8,24},{12,28},{16,0},{20,4},{24,8},{28,12},{1,17},{... | collective-permute-start | bytes 442376 | tf_op jit(solution)/shard_map/ppermute | solution.py:436
  29.3 13.7 %collective-permute-start.9 = (bf16[2,96,384]{2,1,0:T(8,128)(2,1)S(1)}, bf16[2,96,384]{2,1,0:T(8,128)(2,1)S(1)}, u32[]{:S(2)}, u32[]{:S(2)}) collective-permute-start(bf16[2,96,384]{2,1,0:T(8,128)(2,1)S(1)} %pad_maximum_fusion.23), channel_id=1, source_target_pairs={{0,16},{4,20},{8,24},{12,28},{16,0},{20,4},{24,8},{28,12},{1,17},{... | collective-permute-start | bytes 442376 | tf_op jit(solution)/shard_map/ppermute | solution.py:436
  36.6 8.0 %collective-permute-start.15 = (bf16[2,2,48,384]{3,2,1,0:T(8,128)(2,1)S(1)}, bf16[2,2,48,384]{3,2,1,0:T(8,128)(2,1)S(1)}, u32[]{:S(2)}, u32[]{:S(2)}) collective-permute-start(bf16[2,2,48,384]{3,2,1,0:T(8,128)(2,1)S(1)} %pad_maximum_fusion.24), channel_id=1, source_target_pairs={{0,4},{4,0},{8,12},{12,8},{16,20},{20,16},{24,28},{28,24},{1,5},{5... | collective-permute-start | bytes 442376 | tf_op jit(solution)/shard_map/ppermute | solution.py:436
  38.2 8.0 %collective-permute-start.5 = (bf16[2,2,48,384]{3,2,1,0:T(8,128)(2,1)S(1)}, bf16[2,2,48,384]{3,2,1,0:T(8,128)(2,1)S(1)}, u32[]{:S(2)}, u32[]{:S(2)}) collective-permute-start(bf16[2,2,48,384]{3,2,1,0:T(8,128)(2,1)S(1)} %pad_maximum_fusion.22), channel_id=1, source_target_pairs={{0,4},{4,0},{8,12},{12,8},{16,20},{20,16},{24,28},{28,24},{1,5},{5... | collective-permute-start | bytes 442376 | tf_op jit(solution)/shard_map/ppermute | solution.py:436
  41.4 10.6 %collective-permute-start.20 = (bf16[2,2,96,384]{3,2,1,0:T(8,128)(2,1)S(1)}, bf16[2,2,96,384]{3,2,1,0:T(8,128)(2,1)S(1)}, u32[]{:S(2)}, u32[]{:S(2)}) collective-permute-start(bf16[2,2,96,384]{3,2,1,0:T(8,128)(2,1)S(1)} %pad_maximum_fusion.20), channel_id=1, source_target_pairs={{0,4},{4,0},{8,12},{12,8},{16,20},{20,16},{24,28},{28,24},{1,5},{5... | collective-permute-start | bytes 884744 | tf_op jit(solution)/shard_map/ppermute | solution.py:436
  43.1 13.0 %collective-permute-start.10 = (bf16[2,2,96,384]{3,2,1,0:T(8,128)(2,1)S(1)}, bf16[2,2,96,384]{3,2,1,0:T(8,128)(2,1)S(1)}, u32[]{:S(2)}, u32[]{:S(2)}) collective-permute-start(bf16[2,2,96,384]{3,2,1,0:T(8,128)(2,1)S(1)} %pad_maximum_fusion.18), channel_id=1, source_target_pairs={{0,4},{4,0},{8,12},{12,8},{16,20},{20,16},{24,28},{28,24},{1,5},{5... | collective-permute-start | bytes 884744 | tf_op jit(solution)/shard_map/ppermute | solution.py:436
  44.7 13.1 %collective-permute-start.16 = (bf16[2,2,2,48,384]{4,3,2,1,0:T(8,128)(2,1)S(1)}, bf16[2,2,2,48,384]{4,3,2,1,0:T(8,128)(2,1)S(1)}, u32[]{:S(2)}, u32[]{:S(2)}) collective-permute-start(bf16[2,2,2,48,384]{4,3,2,1,0:T(8,128)(2,1)S(1)} %pad_maximum_fusion.19), channel_id=1, source_target_pairs={{0,2},{1,3},{2,0},{3,1},{4,6},{5,7},{6,4},{7,5},{8,10},{9,11},{10,... | collective-permute-start | bytes 884744 | tf_op jit(solution)/shard_map/ppermute | solution.py:436
  46.4 14.7 %collective-permute-start.6 = (bf16[2,2,2,48,384]{4,3,0,2,1:T(8,128)(2,1)S(1)}, bf16[2,2,2,48,384]{4,3,0,2,1:T(8,128)(2,1)S(1)}, u32[]{:S(2)}, u32[]{:S(2)}) collective-permute-start(bf16[2,2,2,48,384]{4,3,0,2,1:T(8,128)(2,1)S(1)} %pad_maximum_fusion.17), channel_id=1, source_target_pairs={{0,2},{1,3},{2,0},{3,1},{4,6},{5,7},{6,4},{7,5},{8,10},{9,11},{10,... | collective-permute-start | bytes 884744 | tf_op jit(solution)/shard_map/ppermute | solution.py:436
  52.2 21.5 %collective-permute-start.21 = (bf16[2,2,2,96,384]{4,3,2,1,0:T(8,128)(2,1)S(1)}, bf16[2,2,2,96,384]{4,3,2,1,0:T(8,128)(2,1)S(1)}, u32[]{:S(2)}, u32[]{:S(2)}) collective-permute-start(bf16[2,2,2,96,384]{4,3,2,1,0:T(8,128)(2,1)S(1)} %pad_maximum_fusion.13), channel_id=1, source_target_pairs={{0,2},{1,3},{2,0},{3,1},{4,6},{5,7},{6,4},{7,5},{8,10},{9,11},{10,... | collective-permute-start | bytes 1769480 | tf_op jit(solution)/shard_map/ppermute | solution.py:436
  56.2 27.4 %collective-permute-start.11 = (bf16[2,2,2,96,384]{4,3,0,2,1:T(8,128)(2,1)S(1)}, bf16[2,2,2,96,384]{4,3,0,2,1:T(8,128)(2,1)S(1)}, u32[]{:S(2)}, u32[]{:S(2)}) collective-permute-start(bf16[2,2,2,96,384]{4,3,0,2,1:T(8,128)(2,1)S(1)} %pad_maximum_fusion.11), channel_id=1, source_target_pairs={{0,2},{1,3},{2,0},{3,1},{4,6},{5,7},{6,4},{7,5},{8,10},{9,11},{10,... | collective-permute-start | bytes 1769480 | tf_op jit(solution)/shard_map/ppermute | solution.py:436
  58.0 26.0 %collective-permute-start.17 = (bf16[2,2,2,2,48,384]{5,4,3,2,1,0:T(8,128)(2,1)S(1)}, bf16[2,2,2,2,48,384]{5,4,3,2,1,0:T(8,128)(2,1)S(1)}, u32[]{:S(2)}, u32[]{:S(2)}) collective-permute-start(bf16[2,2,2,2,48,384]{5,4,3,2,1,0:T(8,128)(2,1)S(1)} %pad_maximum_fusion.12), channel_id=1, source_target_pairs={{0,1},{1,0},{2,3},{3,2},{4,5},{5,4},{6,7},{7,6},{8,9},{9,8},{10,11... | collective-permute-start | bytes 1769480 | tf_op jit(solution)/shard_map/ppermute | solution.py:436
  61.2 25.0 %collective-permute-start.7 = (bf16[2,2,2,2,48,384]{5,4,1,3,2,0:T(8,128)(2,1)S(1)}, bf16[2,2,2,2,48,384]{5,4,1,3,2,0:T(8,128)(2,1)S(1)}, u32[]{:S(2)}, u32[]{:S(2)}) collective-permute-start(bf16[2,2,2,2,48,384]{5,4,1,3,2,0:T(8,128)(2,1)S(1)} %pad_maximum_fusion.10), channel_id=1, source_target_pairs={{0,1},{1,0},{2,3},{3,2},{4,5},{5,4},{6,7},{7,6},{8,9},{9,8},{10,11... | collective-permute-start | bytes 1769480 | tf_op jit(solution)/shard_map/ppermute | solution.py:436
  74.0 26.2 %collective-permute-start.22 = (bf16[2,2,2,2,96,384]{5,4,3,2,1,0:T(8,128)(2,1)S(1)}, bf16[2,2,2,2,96,384]{5,4,3,2,1,0:T(8,128)(2,1)S(1)}, u32[]{:S(2)}, u32[]{:S(2)}) collective-permute-start(bf16[2,2,2,2,96,384]{5,4,3,2,1,0:T(8,128)(2,1)S(1)} %pad_maximum_fusion.4), channel_id=1, source_target_pairs={{0,1},{1,0},{2,3},{3,2},{4,5},{5,4},{6,7},{7,6},{8,9},{9,8},{10,11... | collective-permute-start | bytes 3538952 | tf_op jit(solution)/shard_map/ppermute | solution.py:436
  83.9 19.8 %collective-permute-start.12 = (bf16[2,2,2,2,96,384]{5,4,1,3,2,0:T(8,128)(2,1)S(1)}, bf16[2,2,2,2,96,384]{5,4,1,3,2,0:T(8,128)(2,1)S(1)}, u32[]{:S(2)}, u32[]{:S(2)}) collective-permute-start(bf16[2,2,2,2,96,384]{5,4,1,3,2,0:T(8,128)(2,1)S(1)} %pad_maximum_fusion.3), channel_id=1, source_target_pairs={{0,1},{1,0},{2,3},{3,2},{4,5},{5,4},{6,7},{7,6},{8,9},{9,8},{10,11... | collective-permute-start | bytes 3538952 | tf_op jit(solution)/shard_map/ppermute | solution.py:436
  230.7 4.7 %collective-permute-start.54 = (f32[2,8,1536]{2,1,0:T(8,128)S(1)}, f32[2,8,1536]{2,1,0:T(8,128)S(1)}, u32[]{:S(2)}, u32[]{:S(2)}) collective-permute-start(f32[2,8,1536]{2,1,0:T(8,128)S(1)} %pad_maximum_fusion.31), channel_id=1, source_target_pairs={{0,8},{4,12},{8,0},{12,4},{16,24},{20,28},{24,16},{28,20},{1,9},{5... | collective-permute-start | bytes 294920 | tf_op jit(solution)/shard_map/ppermute | solution.py:436
  232.7 59.1 %collective-permute-start.37 = (bf16[2,2,2,2,96,384]{5,4,3,2,1,0:T(8,128)(2,1)S(1)}, bf16[2,2,2,2,96,384]{5,4,3,2,1,0:T(8,128)(2,1)S(1)}, u32[]{:S(2)}, u32[]{:S(2)}) collective-permute-start(bf16[2,2,2,2,96,384]{5,4,3,2,1,0:T(8,128)(2,1)S(1)} %select_bitcast_fusion.1), channel_id=1, source_target_pairs={{0,1},{1,0},{2,3},{3,2},{4,5},{5,4},{6,7},{7,6},{8,9},{9,8},{10,11... | collective-permute-start | bytes 3538952 | tf_op jit(solution)/shard_map/ppermute | solution.py:436
  235.2 59.4 %collective-permute-start.44 = (bf16[2,2,2,2,96,384]{5,4,3,2,1,0:T(8,128)(2,1)S(1)}, bf16[2,2,2,2,96,384]{5,4,3,2,1,0:T(8,128)(2,1)S(1)}, u32[]{:S(2)}, u32[]{:S(2)}) collective-permute-start(bf16[2,2,2,2,96,384]{5,4,3,2,1,0:T(8,128)(2,1)S(1)} %select_bitcast_fusion), channel_id=1, source_target_pairs={{0,1},{1,0},{2,3},{3,2},{4,5},{5,4},{6,7},{7,6},{8,9},{9,8},{10,11... | collective-permute-start | bytes 3538952 | tf_op jit(solution)/shard_map/ppermute | solution.py:436
  235.4 11.8 %collective-permute-start.55 = (f32[2,8,1536]{2,1,0:T(8,128)S(1)}, f32[2,8,1536]{2,1,0:T(8,128)S(1)}, u32[]{:S(2)}, u32[]{:S(2)}) collective-permute-start(f32[2,8,1536]{2,1,0:T(8,128)S(1)} %fusion.91), channel_id=1, source_target_pairs={{0,16},{4,20},{8,24},{12,28},{16,0},{20,4},{24,8},{28,12},{1,17},{... | collective-permute-start | bytes 294920 | tf_op jit(solution)/shard_map/ppermute | solution.py:436
  247.2 4.7 %collective-permute-start.56 = (f32[2,8,1536]{2,1,0:T(8,128)S(1)}, f32[2,8,1536]{2,1,0:T(8,128)S(1)}, u32[]{:S(2)}, u32[]{:S(2)}) collective-permute-start(f32[2,8,1536]{2,1,0:T(8,128)S(1)} %fusion.110), channel_id=1, source_target_pairs={{0,4},{4,0},{8,12},{12,8},{16,20},{20,16},{24,28},{28,24},{1,5},{5... | collective-permute-start | bytes 294920 | tf_op jit(solution)/shard_map/ppermute | solution.py:436
  247.4 12.4 %collective-permute-start.23 = (bf16[2,2,2,2,48,384]{5,4,3,2,1,0:T(8,128)(2,1)S(1)}, bf16[2,2,2,2,48,384]{5,4,3,2,1,0:T(8,128)(2,1)S(1)}, u32[]{:S(2)}, u32[]{:S(2)}) collective-permute-start(bf16[2,2,2,2,48,384]{5,4,3,2,1,0:T(8,128)(2,1)S(1)} %select_bitcast_fusion.7), channel_id=1, source_target_pairs={{0,1},{1,0},{2,3},{3,2},{4,5},{5,4},{6,7},{7,6},{8,9},{9,8},{10,11... | collective-permute-start | bytes 1769480 | tf_op jit(solution)/shard_map/ppermute | solution.py:436
  251.9 4.7 %collective-permute-start.57 = (f32[2,8,1536]{2,1,0:T(8,128)S(1)}, f32[2,8,1536]{2,1,0:T(8,128)S(1)}, u32[]{:S(2)}, u32[]{:S(2)}) collective-permute-start(f32[2,8,1536]{2,1,0:T(8,128)S(1)} %add.323), channel_id=1, source_target_pairs={{0,2},{1,3},{2,0},{3,1},{4,6},{5,7},{6,4},{7,5},{8,10},{9,11},{10,... | collective-permute-start | bytes 294920 | tf_op jit(solution)/shard_map/ppermute | solution.py:436
  256.6 1.4 collective-permute-start.58
  256.8 3.4 collective-permute-start.30
  260.0 9.9 %collective-permute-start.24 = (bf16[2,2,2,48,384]{4,3,2,1,0:T(8,128)(2,1)S(1)}, bf16[2,2,2,48,384]{4,3,2,1,0:T(8,128)(2,1)S(1)}, u32[]{:S(2)}, u32[]{:S(2)}) collective-permute-start(bf16[2,2,2,48,384]{4,3,2,1,0:T(8,128)(2,1)S(1)} %fusion.35), channel_id=1, source_target_pairs={{0,2},{1,3},{2,0},{3,1},{4,6},{5,7},{6,4},{7,5},{8,10},{9,11},{10,... | collective-permute-start | bytes 884744 | tf_op jit(solution)/shard_map/ppermute | solution.py:436
  260.4 15.1 %collective-permute-start.31 = (bf16[2,2,2,48,384]{4,3,2,1,0:T(8,128)(2,1)S(1)}, bf16[2,2,2,48,384]{4,3,2,1,0:T(8,128)(2,1)S(1)}, u32[]{:S(2)}, u32[]{:S(2)}) collective-permute-start(bf16[2,2,2,48,384]{4,3,2,1,0:T(8,128)(2,1)S(1)} %fusion.36), channel_id=1, source_target_pairs={{0,2},{1,3},{2,0},{3,1},{4,6},{5,7},{6,4},{7,5},{8,10},{9,11},{10,... | collective-permute-start | bytes 884744 | tf_op jit(solution)/shard_map/ppermute | solution.py:436
  270.1 5.7 %collective-permute-start.25 = (bf16[2,2,48,384]{3,2,1,0:T(8,128)(2,1)S(1)}, bf16[2,2,48,384]{3,2,1,0:T(8,128)(2,1)S(1)}, u32[]{:S(2)}, u32[]{:S(2)}) collective-permute-start(bf16[2,2,48,384]{3,2,1,0:T(8,128)(2,1)S(1)} %fusion.46), channel_id=1, source_target_pairs={{0,4},{4,0},{8,12},{12,8},{16,20},{20,16},{24,28},{28,24},{1,5},{5... | collective-permute-start | bytes 442376 | tf_op jit(solution)/shard_map/ppermute | solution.py:436
  275.6 5.2 %collective-permute-start.32 = (bf16[2,2,48,384]{3,2,1,0:T(8,128)(2,1)S(1)}, bf16[2,2,48,384]{3,2,1,0:T(8,128)(2,1)S(1)}, u32[]{:S(2)}, u32[]{:S(2)}) collective-permute-start(bf16[2,2,48,384]{3,2,1,0:T(8,128)(2,1)S(1)} %fusion.47), channel_id=1, source_target_pairs={{0,4},{4,0},{8,12},{12,8},{16,20},{20,16},{24,28},{28,24},{1,5},{5... | collective-permute-start | bytes 442376 | tf_op jit(solution)/shard_map/ppermute | solution.py:436
  275.8 6.1 %collective-permute-start.26 = (bf16[2,48,384]{2,1,0:T(8,128)(2,1)S(1)}, bf16[2,48,384]{2,1,0:T(8,128)(2,1)S(1)}, u32[]{:S(2)}, u32[]{:S(2)}) collective-permute-start(bf16[2,48,384]{2,1,0:T(8,128)(2,1)S(1)} %fusion.56), channel_id=1, source_target_pairs={{0,16},{4,20},{8,24},{12,28},{16,0},{20,4},{24,8},{28,12},{1,17},{... | collective-permute-start | bytes 221192 | tf_op jit(solution)/shard_map/ppermute | solution.py:436
  280.9 6.2 %collective-permute-start.33 = (bf16[2,48,384]{2,1,0:T(8,128)(2,1)S(1)}, bf16[2,48,384]{2,1,0:T(8,128)(2,1)S(1)}, u32[]{:S(2)}, u32[]{:S(2)}) collective-permute-start(bf16[2,48,384]{2,1,0:T(8,128)(2,1)S(1)} %fusion.57), channel_id=1, source_target_pairs={{0,16},{4,20},{8,24},{12,28},{16,0},{20,4},{24,8},{28,12},{1,17},{... | collective-permute-start | bytes 221192 | tf_op jit(solution)/shard_map/ppermute | solution.py:436
  282.0 5.3 %collective-permute-start.27 = (bf16[48,384]{1,0:T(8,128)(2,1)S(1)}, bf16[48,384]{1,0:T(8,128)(2,1)S(1)}, u32[]{:S(2)}, u32[]{:S(2)}) collective-permute-start(bf16[48,384]{1,0:T(8,128)(2,1)S(1)} %fusion.64), channel_id=1, source_target_pairs={{0,8},{4,12},{8,0},{12,4},{16,24},{20,28},{24,16},{28,20},{1,9},{5... | collective-permute-start | bytes 110600 | tf_op jit(solution)/shard_map/ppermute | solution.py:436
  287.1 4.0 collective-permute-start.34
  287.3 9.3 %collective-permute-start.28 = (bf16[48,384]{1,0:T(8,128)(2,1)S(1)}, bf16[48,384]{1,0:T(8,128)(2,1)S(1)}, u32[]{:S(2)}, u32[]{:S(2)}) collective-permute-start(bf16[48,384]{1,0:T(8,128)(2,1)S(1)} %fusion.63), channel_id=1, source_target_pairs={{0,2},{1,3},{2,0},{3,1},{4,6},{5,7},{6,4},{7,5},{8,10},{9,11},{10,... | collective-permute-start | bytes 110600 | tf_op jit(solution)/shard_map/ppermute | solution.py:436
  291.2 5.5 %collective-permute-start.35 = (bf16[48,384]{1,0:T(8,128)(2,1)S(1)}, bf16[48,384]{1,0:T(8,128)(2,1)S(1)}, u32[]{:S(2)}, u32[]{:S(2)}) collective-permute-start(bf16[48,384]{1,0:T(8,128)(2,1)S(1)} %fusion.62), channel_id=1, source_target_pairs={{0,2},{1,3},{2,0},{3,1},{4,6},{5,7},{6,4},{7,5},{8,10},{9,11},{10,... | collective-permute-start | bytes 110600 | tf_op jit(solution)/shard_map/ppermute | solution.py:436
  293.1 16.5 %collective-permute-start.38 = (bf16[2,2,2,96,384]{4,3,2,1,0:T(8,128)(2,1)}, bf16[2,2,2,96,384]{4,3,2,1,0:T(8,128)(2,1)S(1)}, u32[]{:S(2)}, u32[]{:S(2)}) collective-permute-start(bf16[2,2,2,96,384]{4,3,2,1,0:T(8,128)(2,1)} %fusion.14), channel_id=1, source_target_pairs={{0,2},{1,3},{2,0},{3,1},{4,6},{5,7},{6,4},{7,5},{8,10},{9,11},{10,... | collective-permute-start | bytes 1769480 | tf_op jit(solution)/shard_map/ppermute | solution.py:436
  296.1 21.6 %collective-permute-start.45 = (bf16[2,2,2,96,384]{4,3,2,1,0:T(8,128)(2,1)}, bf16[2,2,2,96,384]{4,3,2,1,0:T(8,128)(2,1)S(1)}, u32[]{:S(2)}, u32[]{:S(2)}) collective-permute-start(bf16[2,2,2,96,384]{4,3,2,1,0:T(8,128)(2,1)} %fusion.15), channel_id=1, source_target_pairs={{0,2},{1,3},{2,0},{3,1},{4,6},{5,7},{6,4},{7,5},{8,10},{9,11},{10,... | collective-permute-start | bytes 1769480 | tf_op jit(solution)/shard_map/ppermute | solution.py:436
  296.7 1.3 collective-permute-start.29
  296.8 1.5 collective-permute-start.36
  309.6 8.1 %copy-start.1 = (f32[2,2,2,2,96,384]{5,4,3,2,1,0:T(8,128)S(1)}, f32[2,2,2,2,96,384]{5,4,3,2,1,0:T(8,128)}, u32[]{:S(2)}) copy-start(f32[2,2,2,2,96,384]{5,4,3,2,1,0:T(8,128)} %copy-done) | copy-start | bytes 7077892
  309.8 9.1 %collective-permute-start.39 = (bf16[2,2,96,384]{3,2,1,0:T(8,128)(2,1)S(1)}, bf16[2,2,96,384]{3,2,1,0:T(8,128)(2,1)S(1)}, u32[]{:S(2)}, u32[]{:S(2)}) collective-permute-start(bf16[2,2,96,384]{3,2,1,0:T(8,128)(2,1)S(1)} %fusion.37), channel_id=1, source_target_pairs={{0,4},{4,0},{8,12},{12,8},{16,20},{20,16},{24,28},{28,24},{1,5},{5... | collective-permute-start | bytes 884744 | tf_op jit(solution)/shard_map/ppermute | solution.py:436
  318.0 6.8 %collective-permute-start.46 = (bf16[2,2,96,384]{3,2,1,0:T(8,128)(2,1)S(1)}, bf16[2,2,96,384]{3,2,1,0:T(8,128)(2,1)S(1)}, u32[]{:S(2)}, u32[]{:S(2)}) collective-permute-start(bf16[2,2,96,384]{3,2,1,0:T(8,128)(2,1)S(1)} %fusion.38), channel_id=1, source_target_pairs={{0,4},{4,0},{8,12},{12,8},{16,20},{20,16},{24,28},{28,24},{1,5},{5... | collective-permute-start | bytes 884744 | tf_op jit(solution)/shard_map/ppermute | solution.py:436
  319.1 10.6 %collective-permute-start.40 = (bf16[2,96,384]{2,1,0:T(8,128)(2,1)S(1)}, bf16[2,96,384]{2,1,0:T(8,128)(2,1)S(1)}, u32[]{:S(2)}, u32[]{:S(2)}) collective-permute-start(bf16[2,96,384]{2,1,0:T(8,128)(2,1)S(1)} %fusion.48), channel_id=1, source_target_pairs={{0,16},{4,20},{8,24},{12,28},{16,0},{20,4},{24,8},{28,12},{1,17},{... | collective-permute-start | bytes 442376 | tf_op jit(solution)/shard_map/ppermute | solution.py:436
  324.9 8.0 %collective-permute-start.47 = (bf16[2,96,384]{2,1,0:T(8,128)(2,1)S(1)}, bf16[2,96,384]{2,1,0:T(8,128)(2,1)S(1)}, u32[]{:S(2)}, u32[]{:S(2)}) collective-permute-start(bf16[2,96,384]{2,1,0:T(8,128)(2,1)S(1)} %fusion.49), channel_id=1, source_target_pairs={{0,16},{4,20},{8,24},{12,28},{16,0},{20,4},{24,8},{28,12},{1,17},{... | collective-permute-start | bytes 442376 | tf_op jit(solution)/shard_map/ppermute | solution.py:436
  329.7 4.7 %collective-permute-start.41 = (bf16[96,384]{1,0:T(8,128)(2,1)S(1)}, bf16[96,384]{1,0:T(8,128)(2,1)S(1)}, u32[]{:S(2)}, u32[]{:S(2)}) collective-permute-start(bf16[96,384]{1,0:T(8,128)(2,1)S(1)} %fusion.58), channel_id=1, source_target_pairs={{0,8},{4,12},{8,0},{12,4},{16,24},{20,28},{24,16},{28,20},{1,9},{5... | collective-permute-start | bytes 221192 | tf_op jit(solution)/shard_map/ppermute | solution.py:436
  332.9 4.4 %collective-permute-start.48 = (bf16[96,384]{1,0:T(8,128)(2,1)S(1)}, bf16[96,384]{1,0:T(8,128)(2,1)S(1)}, u32[]{:S(2)}, u32[]{:S(2)}) collective-permute-start(bf16[96,384]{1,0:T(8,128)(2,1)S(1)} %fusion.59), channel_id=1, source_target_pairs={{0,8},{4,12},{8,0},{12,4},{16,24},{20,28},{24,16},{28,20},{1,9},{5... | collective-permute-start | bytes 221192 | tf_op jit(solution)/shard_map/ppermute | solution.py:436
  334.4 5.2 %collective-permute-start.42 = (bf16[96,384]{1,0:T(8,128)(2,1)S(1)}, bf16[96,384]{1,0:T(8,128)(2,1)S(1)}, u32[]{:S(2)}, u32[]{:S(2)}) collective-permute-start(bf16[96,384]{1,0:T(8,128)(2,1)S(1)} %fusion.54), channel_id=1, source_target_pairs={{0,2},{1,3},{2,0},{3,1},{4,6},{5,7},{6,4},{7,5},{8,10},{9,11},{10,... | collective-permute-start | bytes 221192 | tf_op jit(solution)/shard_map/ppermute | solution.py:436
  337.4 4.4 %collective-permute-start.49 = (bf16[96,384]{1,0:T(8,128)(2,1)S(1)}, bf16[96,384]{1,0:T(8,128)(2,1)S(1)}, u32[]{:S(2)}, u32[]{:S(2)}) collective-permute-start(bf16[96,384]{1,0:T(8,128)(2,1)S(1)} %fusion.53), channel_id=1, source_target_pairs={{0,2},{1,3},{2,0},{3,1},{4,6},{5,7},{6,4},{7,5},{8,10},{9,11},{10,... | collective-permute-start | bytes 221192 | tf_op jit(solution)/shard_map/ppermute | solution.py:436
  339.7 2.3 collective-permute-start.43
  341.8 1.4 collective-permute-start.50
  343.4 18.2 %copy-start.2 = (f32[2,2,192,384]{3,2,1,0:T(8,128)S(1)}, f32[2,2,192,384]{3,2,1,0:T(8,128)}, u32[]{:S(2)}) copy-start(f32[2,2,192,384]{3,2,1,0:T(8,128)} %param.27) | copy-start | bytes 3538948
  343.4 18.2 %copy-start.11 = (f32[2,192,384]{2,1,0:T(8,128)S(1)}, f32[2,192,384]{2,1,0:T(8,128)}, u32[]{:S(2)}) copy-start(f32[2,192,384]{2,1,0:T(8,128)} %param.21) | copy-start | bytes 1769476
  346.3 3.7 collective-permute-start.51
  350.6 4.6 %collective-permute-start.52 = (f32[]{:T(128)}, f32[]{:T(128)}, u32[]{:S(2)}, u32[]{:S(2)}) collective-permute-start(f32[]{:T(128)} %add.316), channel_id=1, source_target_pairs={{0,16},{4,20},{8,24},{12,28},{16,0},{20,4},{24,8},{28,12},{1,17},{... | collective-permute-start | bytes 20 | tf_op jit(solution)/shard_map/ppermute | solution.py:436
  355.8 3.7 collective-permute-start.53
  (53 other events, 114.5 us)
